TPU v7x, 32 devices: a whole 2x2x4 slice. The times are simulated.
32 devices in a mesh: slab: 4 (over y, x), grp: 8 (over z, core).
Axes of the slice: x: 2, y: 2, z: 4, core: 2. Of those that a mesh axis runs over, the one named last changes fastest.
Arguments:
- cell_density: float32 [4, 16, 2, 8], P('slab', 'grp'), may hold values from 1 to 10
- cell_slot: int32 [4, 16, 2, 8], P('slab', 'grp'), may hold values from 0 to 7, each once within a row
- neighbours: int32 [4, 16, 2, 6], P('slab', 'grp'), may hold values from -1 to 127, as said below
- face_code: int32 [4, 16, 2, 6], P('slab', 'grp'), may hold values from 0 to 15, as said below
- stiffness: float32 [64, 64], replicated, as said below
- prolong: float32 [8, 64, 64], replicated, as said below
- penalty: float32 [16, 64, 64], replicated, as said below
- fine_rhs: bfloat16 [4, 16, 2, 8, 4096], P('slab', 'grp'), may hold values from -24 to 24
Outputs:
- coarse_correction: float32 [4, 16, 2, 4096], P(None, 'grp')
Inputs may be any that keep to these rules, and one draw needn't show every extreme that they name: `neighbours`: aggregates form a lattice of 4 x 16 x 2; faces in the order -first, +first, -second, +second, -third, +third dimension. Each entry is the number of the lattice neighbour across that face, or -1 where the face lies on the lattice boundary or is a wall; a wall seen from one side is a wall from the other. `face_code`: equal on both sides of every face that is not -1 in neighbours. `cell_slot`: the 8 cells of each aggregate hold each slot once. `stiffness`: Symmetric, each diagonal entry larger than the sum of the magnitudes of the other entries of its row. `prolong`: each diagonal entry larger than the sum of the magnitudes of the other entries of its row. `penalty`: Symmetric, each diagonal entry larger than the sum of the magnitudes of the other entries of its row.
All inputs are finite; a program needn't handle non-finite values.
Results may differ from a plain program's by a relative error of at most 0.0003.
Values sent between devices are 32-bit elements; how exact they have to be, the bound alone decides.
No kernel may reach another device: no remote copies, remote signals or barrier semaphores. Data moves between devices by JAX's collectives and lax.ppermute only.
A program may use at most 128 MiB of HBM per device.

v0:
```python
import jax
import jax.numpy as jnp
from jax import lax
from jax.sharding import PartitionSpec as P

SWEEPS = 8


highest = lax.Precision.HIGHEST


def extended(block, sides, width):
    for axis, dim in sides:
        count = lax.axis_size(axis)
        forward = [(i, i + 1) for i in range(count - 1)]
        backward = [(target, source) for source, target in forward]
        low = lax.ppermute(
            lax.slice_in_dim(block, block.shape[dim] - width, None, axis=dim), axis, forward
        )
        high = lax.ppermute(lax.slice_in_dim(block, 0, width, axis=dim), axis, backward)
        block = jnp.concatenate([low, block, high], axis=dim)
    return block


def assemble(weights, code_hot, templates, penalty):
    kids = templates.shape[0]
    dof_count = templates.shape[1]
    code_count = penalty.shape[0]
    leading = weights.shape[:-1]
    flat_templ = templates.reshape(kids, dof_count * dof_count)
    flat_pen = penalty.reshape(code_count, dof_count * dof_count)
    cell_part = jnp.dot(weights.reshape(-1, kids), flat_templ, precision=highest)
    face_part = jnp.dot(
        jnp.sum(code_hot, axis=-2).reshape(-1, code_count), flat_pen, precision=highest
    )
    diag_flat = (cell_part + face_part).reshape(leading + (dof_count * dof_count,))
    off_flat = (-jnp.dot(code_hot.reshape(-1, code_count), flat_pen, precision=highest)).reshape(
        leading + (6, dof_count * dof_count)
    )
    return (diag_flat, off_flat)


def as_blocks(flat_blocks, dof_count):
    return flat_blocks.reshape(flat_blocks.shape[:-1] + (dof_count, dof_count))


def largest_ratio(diag_flat, off_flat, dof_count):
    diag_blocks = as_blocks(diag_flat, dof_count)
    off_blocks = as_blocks(off_flat, dof_count)
    jacobi = jnp.diagonal(diag_blocks, axis1=-2, axis2=-1)
    totals = jnp.sum(jnp.abs(diag_blocks), axis=-1) + jnp.sum(jnp.abs(off_blocks), axis=(-3, -1))
    return jnp.max(totals / jacobi)


def block_apply(blocks, vector):
    return jnp.einsum("abcij,abcjr->abcir", blocks, vector, precision=highest)


def faces_sum(vector, spread, diag_blocks, off_blocks):
    views = [
        spread[:-2, 1:-1, 1:-1],
        spread[2:, 1:-1, 1:-1],
        spread[1:-1, :-2, 1:-1],
        spread[1:-1, 2:, 1:-1],
        spread[1:-1, 1:-1, :-2],
        spread[1:-1, 1:-1, 2:],
    ]
    result = block_apply(diag_blocks, vector)
    for face in range(6):
        result = result + block_apply(off_blocks[:, :, :, face], views[face].reshape(vector.shape))
    return result


def apply_split(vector, diag_blocks, off_blocks):
    rows_a, rows_b, rows_c, dof_count, rhs_count = vector.shape
    flat = vector.reshape(rows_a, rows_b, rows_c, dof_count * rhs_count)
    framed = extended(flat, (("slab", 0), ("grp", 1)), 1)
    spread = jnp.pad(framed, ((0, 0), (0, 0), (1, 1), (0, 0)))
    return faces_sum(vector, spread, diag_blocks, off_blocks)


def chebyshev(resid, diag_blocks, off_blocks, upper, operator):
    jacobi = jnp.diagonal(diag_blocks, axis1=-2, axis2=-1)[..., None]
    lower = upper / 10.0
    centre_val = 0.5 * (upper + lower)
    half_width = 0.5 * (upper - lower)
    sigma_val = centre_val / half_width
    damping = 1.0 / sigma_val
    update = resid / jacobi / centre_val
    solution = update
    for sweep in range(SWEEPS):
        resid = resid - operator(update, diag_blocks, off_blocks)
        damping_next = 1.0 / (2.0 * sigma_val - damping)
        update = damping_next * damping * update + 2.0 * damping_next / half_width * (
            resid / jacobi
        )
        solution = solution + update
        damping = damping_next
    return solution


def local(cell_density, cell_slot, neighbours, face_code, stiffness, prolong, penalty, fine_rhs):
    rows_a, rows_b, rows_c, kids = cell_density.shape
    dof_count = stiffness.shape[0]
    code_count = penalty.shape[0]
    rhs_count = fine_rhs.shape[-1] // dof_count
    templates = jnp.einsum("sji,jk,skl->sil", prolong, stiffness, prolong, precision=highest)
    mean_rho = jnp.mean(cell_density, axis=3)
    framed = extended(mean_rho, (("slab", 0), ("grp", 1)), 1)
    centre = framed[1:-1, 1:-1]
    spaced = jnp.pad(centre, ((0, 0), (0, 0), (1, 1)))
    others = jnp.stack(
        [
            framed[:-2, 1:-1],
            framed[2:, 1:-1],
            framed[1:-1, :-2],
            framed[1:-1, 2:],
            spaced[:, :, :-2],
            spaced[:, :, 2:],
        ],
        axis=-1,
    )
    present = neighbours >= 0
    face_weight = jnp.where(present, 2.0 / (centre[..., None] + others), jnp.float32(0.0))
    code_hot = (face_code[..., None] == jnp.arange(code_count, dtype=jnp.int32)).astype(
        jnp.float32
    ) * face_weight[..., None]
    onehot = (cell_slot[..., None] == jnp.arange(kids, dtype=jnp.int32)).astype(jnp.float32)
    weights = jnp.einsum("abcq,abcqs->abcs", 1.0 / cell_density, onehot, precision=highest)
    cell_prolong = jnp.einsum("abcqs,sji->abcqji", onehot, prolong, precision=highest)
    cell_rhs = fine_rhs.reshape(rows_a, rows_b, rows_c, kids, dof_count, rhs_count).astype(
        jnp.float32
    )
    coarse_rhs = jnp.einsum("abcqji,abcqjr->abcir", cell_prolong, cell_rhs, precision=highest)
    coarse_rhs = coarse_rhs.reshape(rows_a, rows_b, rows_c, dof_count * rhs_count)
    own_diag, own_off = assemble(weights, code_hot, templates, penalty)
    upper = lax.pmax(largest_ratio(own_diag, own_off, dof_count), ("slab", "grp"))
    resid = coarse_rhs.reshape(coarse_rhs.shape[:-1] + (dof_count, rhs_count))
    solution = chebyshev(
        resid, as_blocks(own_diag, dof_count), as_blocks(own_off, dof_count), upper, apply_split
    )
    local_flat = solution.reshape(solution.shape[:3] + (dof_count * rhs_count,))
    return lax.all_gather(local_flat, "slab", axis=0, tiled=True)


def solution(mesh):
    return jax.shard_map(
        local,
        mesh=mesh,
        in_specs=(
            P("slab", "grp", None, None),
            P("slab", "grp", None, None),
            P("slab", "grp", None, None),
            P("slab", "grp", None, None),
            P(),
            P(),
            P(),
            P("slab", "grp", None, None, None),
        ),
        out_specs=P(None, "grp", None, None),
        check_vma=False,
    )
```

profile of v0, /device:TPU:1, one launch (start us, length us, event | category | flops | bytes accessed | tf_op | source)
XLA Modules:
  0.0 241.2 jit_solution(12470772247066541449)
XLA Ops:
  0.8 3.9 %collective-permute-start = (f32[1,2,2]{2,1,0:T(2,128)S(1)}, f32[1,2,2]{2,1,0:T(2,128)S(1)}, u32[]{:S(2)}, u32[]{:S(2)}) collective-permute-start(f32[1,2,2]{2,1,0:T(2,128)S(1)} %get-tuple-element.60), channel_id=1, source_target_pairs={{0,8},{8,16},{16,24},{1,9},{9,17},{17,25},{2,10},{10,18},{18,26},{... | collective-permute-start | bytes 56 | tf_op jit(solution)/shard_map/ppermute | solution.py:17
  13.4 2.9 %collective-permute-start.3 = (f32[3,1,2]{2,1,0:T(1,128)S(1)}, f32[3,1,2]{2,1,0:T(1,128)S(1)}, u32[]{:S(2)}, u32[]{:S(2)}) collective-permute-start(f32[3,1,2]{2,1,0:T(1,128)S(1)} %get-tuple-element.55), channel_id=1, source_target_pairs={{1,0},{2,1},{3,2},{4,3},{5,4},{6,5},{7,6},{9,8},{10,9},{11,10},{12... | collective-permute-start | bytes 80 | tf_op jit(solution)/shard_map/ppermute | solution.py:20
  16.3 3.1 %collective-permute-start.2 = (f32[3,1,2]{2,1,0:T(1,128)S(1)}, f32[3,1,2]{2,1,0:T(1,128)S(1)}, u32[]{:S(2)}, u32[]{:S(2)}) collective-permute-start(f32[3,1,2]{2,1,0:T(1,128)S(1)} %get-tuple-element.56), channel_id=1, source_target_pairs={{0,1},{1,2},{2,3},{3,4},{4,5},{5,6},{6,7},{8,9},{9,10},{10,11},{11... | collective-permute-start | bytes 80 | tf_op jit(solution)/shard_map/ppermute | solution.py:17
  22.6 4.5 %copy.88 = f32[2,2,64,64]{1,0,3,2:T(2,128)} copy(f32[2,2,64,64]{3,2,1,0:T(8,128)S(1)} %reshape.860) | data formatting | bytes 131072 | tf_op jit(solution)/shard_map/reshape;reshape | solution.py:44
  27.0 2.9 %gather_fusion = f32[64,2,2]{2,1,0:T(2,128)S(1)} fusion(f32[2,2,64,64]{1,0,3,2:T(2,128)} %copy.88, s32[64]{0:T(128)S(1)} %or_bitcast_fusion), kind=kCustom, calls=%fused_computation | custom fusion | bytes 2560 | tf_op jit(solution)/shard_map/jit(diagonal)/gather | solution.py:83
  31.3 41.7 %pmax.7 = f32[]{:T(128)} all-reduce(f32[]{:T(128)} %fusion.76), channel_id=1, replica_groups=mesh['slab'=4,'grp'=8] {'slab','grp'}, use_global_device_ids=true, to_apply=%region_5.6 | all-reduce | flops 1 | bytes 8 | tf_op jit(solution)/shard_map/pmax | solution.py:137
  75.5 3.8 %collective-permute-start.4 = (f32[1,2,2,4096]{3,2,1,0:T(2,128)S(1)}, f32[1,2,2,4096]{3,2,1,0:T(2,128)S(1)}, u32[]{:S(2)}, u32[]{:S(2)}) collective-permute-start(f32[1,2,2,4096]{3,2,1,0:T(2,128)S(1)} %reshape.798), channel_id=1, source_target_pairs={{0,8},{8,16},{16,24},{1,9},{9,17},{17,25},{2,10},{10,18},{18,26},{... | collective-permute-start | bytes 196616 | tf_op jit(solution)/shard_map/ppermute | solution.py:17
  82.3 2.5 %collective-permute-done.5 = f32[1,2,2,4096]{3,2,1,0:T(2,128)S(1)} collective-permute-done((f32[1,2,2,4096]{3,2,1,0:T(2,128)S(1)}, f32[1,2,2,4096]{3,2,1,0:T(2,128)S(1)}, u32[]{:S(2)}, u32[]{:S(2)}) %collective-permute-start.5) | collective-permute-done | bytes 65568 | tf_op jit(solution)/shard_map/ppermute | solution.py:20
  84.9 4.2 %collective-permute-start.7 = (f32[3,1,2,4096]{3,2,1,0:T(2,128)S(1)}, f32[3,1,2,4096]{3,2,1,0:T(2,128)S(1)}, u32[]{:S(2)}, u32[]{:S(2)}) collective-permute-start(f32[3,1,2,4096]{3,2,1,0:T(2,128)S(1)} %get-tuple-element.52), channel_id=1, source_target_pairs={{1,0},{2,1},{3,2},{4,3},{5,4},{6,5},{7,6},{9,8},{10,9},{11,10},{12... | collective-permute-start | bytes 294920 | tf_op jit(solution)/shard_map/ppermute | solution.py:20
  89.1 3.0 %collective-permute-start.6 = (f32[3,1,2,4096]{3,2,1,0:T(2,128)S(1)}, f32[3,1,2,4096]{3,2,1,0:T(2,128)S(1)}, u32[]{:S(2)}, u32[]{:S(2)}) collective-permute-start(f32[3,1,2,4096]{3,2,1,0:T(2,128)S(1)} %get-tuple-element.51), channel_id=1, source_target_pairs={{0,1},{1,2},{2,3},{3,4},{4,5},{5,6},{6,7},{8,9},{9,10},{10,11},{11... | collective-permute-start | bytes 294920 | tf_op jit(solution)/shard_map/ppermute | solution.py:17
  96.2 4.2 %collective-permute-start.8 = (f32[1,2,2,4096]{3,2,1,0:T(2,128)S(1)}, f32[1,2,2,4096]{3,2,1,0:T(2,128)S(1)}, u32[]{:S(2)}, u32[]{:S(2)}) collective-permute-start(f32[1,2,2,4096]{3,2,1,0:T(2,128)S(1)} %reshape.810), channel_id=1, source_target_pairs={{0,8},{8,16},{16,24},{1,9},{9,17},{17,25},{2,10},{10,18},{18,26},{... | collective-permute-start | bytes 196616 | tf_op jit(solution)/shard_map/ppermute | solution.py:17
  102.0 3.5 %collective-permute-done.9 = f32[1,2,2,4096]{3,2,1,0:T(2,128)S(1)} collective-permute-done((f32[1,2,2,4096]{3,2,1,0:T(2,128)S(1)}, f32[1,2,2,4096]{3,2,1,0:T(2,128)S(1)}, u32[]{:S(2)}, u32[]{:S(2)}) %collective-permute-start.9) | collective-permute-done | bytes 65568 | tf_op jit(solution)/shard_map/ppermute | solution.py:20
  107.6 5.7 %collective-permute-start.10 = (f32[3,1,2,4096]{3,2,1,0:T(2,128)S(1)}, f32[3,1,2,4096]{3,2,1,0:T(2,128)S(1)}, u32[]{:S(2)}, u32[]{:S(2)}) collective-permute-start(f32[3,1,2,4096]{3,2,1,0:T(2,128)S(1)} %get-tuple-element.47), channel_id=1, source_target_pairs={{0,1},{1,2},{2,3},{3,4},{4,5},{5,6},{6,7},{8,9},{9,10},{10,11},{11... | collective-permute-start | bytes 294920 | tf_op jit(solution)/shard_map/ppermute | solution.py:17
  117.2 3.1 %collective-permute-start.12 = (f32[1,2,2,4096]{3,2,1,0:T(2,128)S(1)}, f32[1,2,2,4096]{3,2,1,0:T(2,128)S(1)}, u32[]{:S(2)}, u32[]{:S(2)}) collective-permute-start(f32[1,2,2,4096]{3,2,1,0:T(2,128)S(1)} %reshape.817), channel_id=1, source_target_pairs={{0,8},{8,16},{16,24},{1,9},{9,17},{17,25},{2,10},{10,18},{18,26},{... | collective-permute-start | bytes 196616 | tf_op jit(solution)/shard_map/ppermute | solution.py:17
  121.9 3.4 %collective-permute-done.13 = f32[1,2,2,4096]{3,2,1,0:T(2,128)S(1)} collective-permute-done((f32[1,2,2,4096]{3,2,1,0:T(2,128)S(1)}, f32[1,2,2,4096]{3,2,1,0:T(2,128)S(1)}, u32[]{:S(2)}, u32[]{:S(2)}) %collective-permute-start.13) | collective-permute-done | bytes 65568 | tf_op jit(solution)/shard_map/ppermute | solution.py:20
  127.3 5.7 %collective-permute-start.14 = (f32[3,1,2,4096]{3,2,1,0:T(2,128)S(1)}, f32[3,1,2,4096]{3,2,1,0:T(2,128)S(1)}, u32[]{:S(2)}, u32[]{:S(2)}) collective-permute-start(f32[3,1,2,4096]{3,2,1,0:T(2,128)S(1)} %get-tuple-element.43), channel_id=1, source_target_pairs={{0,1},{1,2},{2,3},{3,4},{4,5},{5,6},{6,7},{8,9},{9,10},{10,11},{11... | collective-permute-start | bytes 294920 | tf_op jit(solution)/shard_map/ppermute | solution.py:17
  137.1 2.5 %collective-permute-start.16 = (f32[1,2,2,4096]{3,2,1,0:T(2,128)S(1)}, f32[1,2,2,4096]{3,2,1,0:T(2,128)S(1)}, u32[]{:S(2)}, u32[]{:S(2)}) collective-permute-start(f32[1,2,2,4096]{3,2,1,0:T(2,128)S(1)} %reshape.824), channel_id=1, source_target_pairs={{0,8},{8,16},{16,24},{1,9},{9,17},{17,25},{2,10},{10,18},{18,26},{... | collective-permute-start | bytes 196616 | tf_op jit(solution)/shard_map/ppermute | solution.py:17
  141.3 3.4 %collective-permute-done.17 = f32[1,2,2,4096]{3,2,1,0:T(2,128)S(1)} collective-permute-done((f32[1,2,2,4096]{3,2,1,0:T(2,128)S(1)}, f32[1,2,2,4096]{3,2,1,0:T(2,128)S(1)}, u32[]{:S(2)}, u32[]{:S(2)}) %collective-permute-start.17) | collective-permute-done | bytes 65568 | tf_op jit(solution)/shard_map/ppermute | solution.py:20
  146.7 5.7 %collective-permute-start.18 = (f32[3,1,2,4096]{3,2,1,0:T(2,128)S(1)}, f32[3,1,2,4096]{3,2,1,0:T(2,128)S(1)}, u32[]{:S(2)}, u32[]{:S(2)}) collective-permute-start(f32[3,1,2,4096]{3,2,1,0:T(2,128)S(1)} %get-tuple-element.39), channel_id=1, source_target_pairs={{0,1},{1,2},{2,3},{3,4},{4,5},{5,6},{6,7},{8,9},{9,10},{10,11},{11... | collective-permute-start | bytes 294920 | tf_op jit(solution)/shard_map/ppermute | solution.py:17
  156.5 2.5 %collective-permute-start.20 = (f32[1,2,2,4096]{3,2,1,0:T(2,128)S(1)}, f32[1,2,2,4096]{3,2,1,0:T(2,128)S(1)}, u32[]{:S(2)}, u32[]{:S(2)}) collective-permute-start(f32[1,2,2,4096]{3,2,1,0:T(2,128)S(1)} %reshape.831), channel_id=1, source_target_pairs={{0,8},{8,16},{16,24},{1,9},{9,17},{17,25},{2,10},{10,18},{18,26},{... | collective-permute-start | bytes 196616 | tf_op jit(solution)/shard_map/ppermute | solution.py:17
  160.6 3.4 %collective-permute-done.21 = f32[1,2,2,4096]{3,2,1,0:T(2,128)S(1)} collective-permute-done((f32[1,2,2,4096]{3,2,1,0:T(2,128)S(1)}, f32[1,2,2,4096]{3,2,1,0:T(2,128)S(1)}, u32[]{:S(2)}, u32[]{:S(2)}) %collective-permute-start.21) | collective-permute-done | bytes 65568 | tf_op jit(solution)/shard_map/ppermute | solution.py:20
  166.0 5.7 %collective-permute-start.22 = (f32[3,1,2,4096]{3,2,1,0:T(2,128)S(1)}, f32[3,1,2,4096]{3,2,1,0:T(2,128)S(1)}, u32[]{:S(2)}, u32[]{:S(2)}) collective-permute-start(f32[3,1,2,4096]{3,2,1,0:T(2,128)S(1)} %get-tuple-element.35), channel_id=1, source_target_pairs={{0,1},{1,2},{2,3},{3,4},{4,5},{5,6},{6,7},{8,9},{9,10},{10,11},{11... | collective-permute-start | bytes 294920 | tf_op jit(solution)/shard_map/ppermute | solution.py:17
  175.8 2.5 %collective-permute-start.24 = (f32[1,2,2,4096]{3,2,1,0:T(2,128)S(1)}, f32[1,2,2,4096]{3,2,1,0:T(2,128)S(1)}, u32[]{:S(2)}, u32[]{:S(2)}) collective-permute-start(f32[1,2,2,4096]{3,2,1,0:T(2,128)S(1)} %reshape.838), channel_id=1, source_target_pairs={{0,8},{8,16},{16,24},{1,9},{9,17},{17,25},{2,10},{10,18},{18,26},{... | collective-permute-start | bytes 196616 | tf_op jit(solution)/shard_map/ppermute | solution.py:17
  180.0 3.4 %collective-permute-done.25 = f32[1,2,2,4096]{3,2,1,0:T(2,128)S(1)} collective-permute-done((f32[1,2,2,4096]{3,2,1,0:T(2,128)S(1)}, f32[1,2,2,4096]{3,2,1,0:T(2,128)S(1)}, u32[]{:S(2)}, u32[]{:S(2)}) %collective-permute-start.25) | collective-permute-done | bytes 65568 | tf_op jit(solution)/shard_map/ppermute | solution.py:20
  185.4 6.0 %collective-permute-start.26 = (f32[3,1,2,4096]{3,2,1,0:T(2,128)S(1)}, f32[3,1,2,4096]{3,2,1,0:T(2,128)S(1)}, u32[]{:S(2)}, u32[]{:S(2)}) collective-permute-start(f32[3,1,2,4096]{3,2,1,0:T(2,128)S(1)} %get-tuple-element.31), channel_id=1, source_target_pairs={{0,1},{1,2},{2,3},{3,4},{4,5},{5,6},{6,7},{8,9},{9,10},{10,11},{11... | collective-permute-start | bytes 294920 | tf_op jit(solution)/shard_map/ppermute | solution.py:17
  195.2 2.5 %collective-permute-start.28 = (f32[1,2,2,4096]{3,2,1,0:T(2,128)S(1)}, f32[1,2,2,4096]{3,2,1,0:T(2,128)S(1)}, u32[]{:S(2)}, u32[]{:S(2)}) collective-permute-start(f32[1,2,2,4096]{3,2,1,0:T(2,128)S(1)} %reshape.845), channel_id=1, source_target_pairs={{0,8},{8,16},{16,24},{1,9},{9,17},{17,25},{2,10},{10,18},{18,26},{... | collective-permute-start | bytes 196616 | tf_op jit(solution)/shard_map/ppermute | solution.py:17
  199.3 3.4 %collective-permute-done.29 = f32[1,2,2,4096]{3,2,1,0:T(2,128)S(1)} collective-permute-done((f32[1,2,2,4096]{3,2,1,0:T(2,128)S(1)}, f32[1,2,2,4096]{3,2,1,0:T(2,128)S(1)}, u32[]{:S(2)}, u32[]{:S(2)}) %collective-permute-start.29) | collective-permute-done | bytes 65568 | tf_op jit(solution)/shard_map/ppermute | solution.py:20
  204.7 5.7 %collective-permute-start.30 = (f32[3,1,2,4096]{3,2,1,0:T(2,128)S(1)}, f32[3,1,2,4096]{3,2,1,0:T(2,128)S(1)}, u32[]{:S(2)}, u32[]{:S(2)}) collective-permute-start(f32[3,1,2,4096]{3,2,1,0:T(2,128)S(1)} %get-tuple-element.27), channel_id=1, source_target_pairs={{0,1},{1,2},{2,3},{3,4},{4,5},{5,6},{6,7},{8,9},{9,10},{10,11},{11... | collective-permute-start | bytes 294920 | tf_op jit(solution)/shard_map/ppermute | solution.py:17
  214.5 2.5 %collective-permute-start.32 = (f32[1,2,2,4096]{3,2,1,0:T(2,128)S(1)}, f32[1,2,2,4096]{3,2,1,0:T(2,128)S(1)}, u32[]{:S(2)}, u32[]{:S(2)}) collective-permute-start(f32[1,2,2,4096]{3,2,1,0:T(2,128)S(1)} %reshape.852), channel_id=1, source_target_pairs={{0,8},{8,16},{16,24},{1,9},{9,17},{17,25},{2,10},{10,18},{18,26},{... | collective-permute-start | bytes 196616 | tf_op jit(solution)/shard_map/ppermute | solution.py:17
  218.7 3.4 %collective-permute-done.33 = f32[1,2,2,4096]{3,2,1,0:T(2,128)S(1)} collective-permute-done((f32[1,2,2,4096]{3,2,1,0:T(2,128)S(1)}, f32[1,2,2,4096]{3,2,1,0:T(2,128)S(1)}, u32[]{:S(2)}, u32[]{:S(2)}) %collective-permute-start.33) | collective-permute-done | bytes 65568 | tf_op jit(solution)/shard_map/ppermute | solution.py:20
  224.1 5.7 %collective-permute-start.34 = (f32[3,1,2,4096]{3,2,1,0:T(2,128)S(1)}, f32[3,1,2,4096]{3,2,1,0:T(2,128)S(1)}, u32[]{:S(2)}, u32[]{:S(2)}) collective-permute-start(f32[3,1,2,4096]{3,2,1,0:T(2,128)S(1)} %get-tuple-element.23), channel_id=1, source_target_pairs={{0,1},{1,2},{2,3},{3,4},{4,5},{5,6},{6,7},{8,9},{9,10},{10,11},{11... | collective-permute-start | bytes 294920 | tf_op jit(solution)/shard_map/ppermute | solution.py:17
  233.9 6.6 %all_gather.3 = f32[4,2,2,4096]{3,2,1,0:T(2,128)S(1)} all-gather(f32[1,2,2,4096]{3,2,1,0:T(2,128)S(1)} %reshape.859), channel_id=1, replica_groups=mesh['slab'=4,'grp'=8] {'slab'}, dimensions={0}, use_global_device_ids=true | all-gather | bytes 327680 | tf_op jit(solution)/shard_map/all_gather | solution.py:143
  (258 shorter events, 73.7 us)
Async XLA Ops:
  0.8 12.4 %collective-permute-start = (f32[1,2,2]{2,1,0:T(2,128)S(1)}, f32[1,2,2]{2,1,0:T(2,128)S(1)}, u32[]{:S(2)}, u32[]{:S(2)}) collective-permute-start(f32[1,2,2]{2,1,0:T(2,128)S(1)} %get-tuple-element.60), channel_id=1, source_target_pairs={{0,8},{8,16},{16,24},{1,9},{9,17},{17,25},{2,10},{10,18},{18,26},{... | collective-permute-start | bytes 56 | tf_op jit(solution)/shard_map/ppermute | solution.py:17
  4.8 8.5 %collective-permute-start.1 = (f32[1,2,2]{2,1,0:T(2,128)S(1)}, f32[1,2,2]{2,1,0:T(2,128)S(1)}, u32[]{:S(2)}, u32[]{:S(2)}) collective-permute-start(f32[1,2,2]{2,1,0:T(2,128)S(1)} %get-tuple-element.60), channel_id=1, source_target_pairs={{8,0},{16,8},{24,16},{9,1},{17,9},{25,17},{10,2},{18,10},{26,18},{... | collective-permute-start | bytes 56 | tf_op jit(solution)/shard_map/ppermute | solution.py:20
  13.4 6.0 %collective-permute-start.3 = (f32[3,1,2]{2,1,0:T(1,128)S(1)}, f32[3,1,2]{2,1,0:T(1,128)S(1)}, u32[]{:S(2)}, u32[]{:S(2)}) collective-permute-start(f32[3,1,2]{2,1,0:T(1,128)S(1)} %get-tuple-element.55), channel_id=1, source_target_pairs={{1,0},{2,1},{3,2},{4,3},{5,4},{6,5},{7,6},{9,8},{10,9},{11,10},{12... | collective-permute-start | bytes 80 | tf_op jit(solution)/shard_map/ppermute | solution.py:20
  75.5 6.8 %collective-permute-start.4 = (f32[1,2,2,4096]{3,2,1,0:T(2,128)S(1)}, f32[1,2,2,4096]{3,2,1,0:T(2,128)S(1)}, u32[]{:S(2)}, u32[]{:S(2)}) collective-permute-start(f32[1,2,2,4096]{3,2,1,0:T(2,128)S(1)} %reshape.798), channel_id=1, source_target_pairs={{0,8},{8,16},{16,24},{1,9},{9,17},{17,25},{2,10},{10,18},{18,26},{... | collective-permute-start | bytes 196616 | tf_op jit(solution)/shard_map/ppermute | solution.py:17
  79.3 5.5 %collective-permute-start.5 = (f32[1,2,2,4096]{3,2,1,0:T(2,128)S(1)}, f32[1,2,2,4096]{3,2,1,0:T(2,128)S(1)}, u32[]{:S(2)}, u32[]{:S(2)}) collective-permute-start(f32[1,2,2,4096]{3,2,1,0:T(2,128)S(1)} %reshape.798), channel_id=1, source_target_pairs={{8,0},{16,8},{24,16},{9,1},{17,9},{25,17},{10,2},{18,10},{26,18},{... | collective-permute-start | bytes 196616 | tf_op jit(solution)/shard_map/ppermute | solution.py:20
  84.9 7.8 %collective-permute-start.7 = (f32[3,1,2,4096]{3,2,1,0:T(2,128)S(1)}, f32[3,1,2,4096]{3,2,1,0:T(2,128)S(1)}, u32[]{:S(2)}, u32[]{:S(2)}) collective-permute-start(f32[3,1,2,4096]{3,2,1,0:T(2,128)S(1)} %get-tuple-element.52), channel_id=1, source_target_pairs={{1,0},{2,1},{3,2},{4,3},{5,4},{6,5},{7,6},{9,8},{10,9},{11,10},{12... | collective-permute-start | bytes 294920 | tf_op jit(solution)/shard_map/ppermute | solution.py:20
  89.1 4.7 %collective-permute-start.6 = (f32[3,1,2,4096]{3,2,1,0:T(2,128)S(1)}, f32[3,1,2,4096]{3,2,1,0:T(2,128)S(1)}, u32[]{:S(2)}, u32[]{:S(2)}) collective-permute-start(f32[3,1,2,4096]{3,2,1,0:T(2,128)S(1)} %get-tuple-element.51), channel_id=1, source_target_pairs={{0,1},{1,2},{2,3},{3,4},{4,5},{5,6},{6,7},{8,9},{9,10},{10,11},{11... | collective-permute-start | bytes 294920 | tf_op jit(solution)/shard_map/ppermute | solution.py:17
  96.2 5.7 %collective-permute-start.8 = (f32[1,2,2,4096]{3,2,1,0:T(2,128)S(1)}, f32[1,2,2,4096]{3,2,1,0:T(2,128)S(1)}, u32[]{:S(2)}, u32[]{:S(2)}) collective-permute-start(f32[1,2,2,4096]{3,2,1,0:T(2,128)S(1)} %reshape.810), channel_id=1, source_target_pairs={{0,8},{8,16},{16,24},{1,9},{9,17},{17,25},{2,10},{10,18},{18,26},{... | collective-permute-start | bytes 196616 | tf_op jit(solution)/shard_map/ppermute | solution.py:17
  100.4 5.2 %collective-permute-start.9 = (f32[1,2,2,4096]{3,2,1,0:T(2,128)S(1)}, f32[1,2,2,4096]{3,2,1,0:T(2,128)S(1)}, u32[]{:S(2)}, u32[]{:S(2)}) collective-permute-start(f32[1,2,2,4096]{3,2,1,0:T(2,128)S(1)} %reshape.810), channel_id=1, source_target_pairs={{8,0},{16,8},{24,16},{9,1},{17,9},{25,17},{10,2},{18,10},{26,18},{... | collective-permute-start | bytes 196616 | tf_op jit(solution)/shard_map/ppermute | solution.py:20
  105.6 8.3 %collective-permute-start.11 = (f32[3,1,2,4096]{3,2,1,0:T(2,128)S(1)}, f32[3,1,2,4096]{3,2,1,0:T(2,128)S(1)}, u32[]{:S(2)}, u32[]{:S(2)}) collective-permute-start(f32[3,1,2,4096]{3,2,1,0:T(2,128)S(1)} %get-tuple-element.48), channel_id=1, source_target_pairs={{1,0},{2,1},{3,2},{4,3},{5,4},{6,5},{7,6},{9,8},{10,9},{11,10},{12... | collective-permute-start | bytes 294920 | tf_op jit(solution)/shard_map/ppermute | solution.py:20
  107.6 7.1 %collective-permute-start.10 = (f32[3,1,2,4096]{3,2,1,0:T(2,128)S(1)}, f32[3,1,2,4096]{3,2,1,0:T(2,128)S(1)}, u32[]{:S(2)}, u32[]{:S(2)}) collective-permute-start(f32[3,1,2,4096]{3,2,1,0:T(2,128)S(1)} %get-tuple-element.47), channel_id=1, source_target_pairs={{0,1},{1,2},{2,3},{3,4},{4,5},{5,6},{6,7},{8,9},{9,10},{10,11},{11... | collective-permute-start | bytes 294920 | tf_op jit(solution)/shard_map/ppermute | solution.py:17
  117.2 4.7 %collective-permute-start.12 = (f32[1,2,2,4096]{3,2,1,0:T(2,128)S(1)}, f32[1,2,2,4096]{3,2,1,0:T(2,128)S(1)}, u32[]{:S(2)}, u32[]{:S(2)}) collective-permute-start(f32[1,2,2,4096]{3,2,1,0:T(2,128)S(1)} %reshape.817), channel_id=1, source_target_pairs={{0,8},{8,16},{16,24},{1,9},{9,17},{17,25},{2,10},{10,18},{18,26},{... | collective-permute-start | bytes 196616 | tf_op jit(solution)/shard_map/ppermute | solution.py:17
  120.3 5.0 %collective-permute-start.13 = (f32[1,2,2,4096]{3,2,1,0:T(2,128)S(1)}, f32[1,2,2,4096]{3,2,1,0:T(2,128)S(1)}, u32[]{:S(2)}, u32[]{:S(2)}) collective-permute-start(f32[1,2,2,4096]{3,2,1,0:T(2,128)S(1)} %reshape.817), channel_id=1, source_target_pairs={{8,0},{16,8},{24,16},{9,1},{17,9},{25,17},{10,2},{18,10},{26,18},{... | collective-permute-start | bytes 196616 | tf_op jit(solution)/shard_map/ppermute | solution.py:20
  125.4 8.2 %collective-permute-start.15 = (f32[3,1,2,4096]{3,2,1,0:T(2,128)S(1)}, f32[3,1,2,4096]{3,2,1,0:T(2,128)S(1)}, u32[]{:S(2)}, u32[]{:S(2)}) collective-permute-start(f32[3,1,2,4096]{3,2,1,0:T(2,128)S(1)} %get-tuple-element.44), channel_id=1, source_target_pairs={{1,0},{2,1},{3,2},{4,3},{5,4},{6,5},{7,6},{9,8},{10,9},{11,10},{12... | collective-permute-start | bytes 294920 | tf_op jit(solution)/shard_map/ppermute | solution.py:20
  127.3 7.4 %collective-permute-start.14 = (f32[3,1,2,4096]{3,2,1,0:T(2,128)S(1)}, f32[3,1,2,4096]{3,2,1,0:T(2,128)S(1)}, u32[]{:S(2)}, u32[]{:S(2)}) collective-permute-start(f32[3,1,2,4096]{3,2,1,0:T(2,128)S(1)} %get-tuple-element.43), channel_id=1, source_target_pairs={{0,1},{1,2},{2,3},{3,4},{4,5},{5,6},{6,7},{8,9},{9,10},{10,11},{11... | collective-permute-start | bytes 294920 | tf_op jit(solution)/shard_map/ppermute | solution.py:17
  137.1 4.1 %collective-permute-start.16 = (f32[1,2,2,4096]{3,2,1,0:T(2,128)S(1)}, f32[1,2,2,4096]{3,2,1,0:T(2,128)S(1)}, u32[]{:S(2)}, u32[]{:S(2)}) collective-permute-start(f32[1,2,2,4096]{3,2,1,0:T(2,128)S(1)} %reshape.824), channel_id=1, source_target_pairs={{0,8},{8,16},{16,24},{1,9},{9,17},{17,25},{2,10},{10,18},{18,26},{... | collective-permute-start | bytes 196616 | tf_op jit(solution)/shard_map/ppermute | solution.py:17
  139.7 5.0 %collective-permute-start.17 = (f32[1,2,2,4096]{3,2,1,0:T(2,128)S(1)}, f32[1,2,2,4096]{3,2,1,0:T(2,128)S(1)}, u32[]{:S(2)}, u32[]{:S(2)}) collective-permute-start(f32[1,2,2,4096]{3,2,1,0:T(2,128)S(1)} %reshape.824), channel_id=1, source_target_pairs={{8,0},{16,8},{24,16},{9,1},{17,9},{25,17},{10,2},{18,10},{26,18},{... | collective-permute-start | bytes 196616 | tf_op jit(solution)/shard_map/ppermute | solution.py:20
  144.7 8.2 %collective-permute-start.19 = (f32[3,1,2,4096]{3,2,1,0:T(2,128)S(1)}, f32[3,1,2,4096]{3,2,1,0:T(2,128)S(1)}, u32[]{:S(2)}, u32[]{:S(2)}) collective-permute-start(f32[3,1,2,4096]{3,2,1,0:T(2,128)S(1)} %get-tuple-element.40), channel_id=1, source_target_pairs={{1,0},{2,1},{3,2},{4,3},{5,4},{6,5},{7,6},{9,8},{10,9},{11,10},{12... | collective-permute-start | bytes 294920 | tf_op jit(solution)/shard_map/ppermute | solution.py:20
  146.7 7.4 %collective-permute-start.18 = (f32[3,1,2,4096]{3,2,1,0:T(2,128)S(1)}, f32[3,1,2,4096]{3,2,1,0:T(2,128)S(1)}, u32[]{:S(2)}, u32[]{:S(2)}) collective-permute-start(f32[3,1,2,4096]{3,2,1,0:T(2,128)S(1)} %get-tuple-element.39), channel_id=1, source_target_pairs={{0,1},{1,2},{2,3},{3,4},{4,5},{5,6},{6,7},{8,9},{9,10},{10,11},{11... | collective-permute-start | bytes 294920 | tf_op jit(solution)/shard_map/ppermute | solution.py:17
  156.5 4.1 %collective-permute-start.20 = (f32[1,2,2,4096]{3,2,1,0:T(2,128)S(1)}, f32[1,2,2,4096]{3,2,1,0:T(2,128)S(1)}, u32[]{:S(2)}, u32[]{:S(2)}) collective-permute-start(f32[1,2,2,4096]{3,2,1,0:T(2,128)S(1)} %reshape.831), channel_id=1, source_target_pairs={{0,8},{8,16},{16,24},{1,9},{9,17},{17,25},{2,10},{10,18},{18,26},{... | collective-permute-start | bytes 196616 | tf_op jit(solution)/shard_map/ppermute | solution.py:17
  159.0 5.0 %collective-permute-start.21 = (f32[1,2,2,4096]{3,2,1,0:T(2,128)S(1)}, f32[1,2,2,4096]{3,2,1,0:T(2,128)S(1)}, u32[]{:S(2)}, u32[]{:S(2)}) collective-permute-start(f32[1,2,2,4096]{3,2,1,0:T(2,128)S(1)} %reshape.831), channel_id=1, source_target_pairs={{8,0},{16,8},{24,16},{9,1},{17,9},{25,17},{10,2},{18,10},{26,18},{... | collective-permute-start | bytes 196616 | tf_op jit(solution)/shard_map/ppermute | solution.py:20
  164.1 8.2 %collective-permute-start.23 = (f32[3,1,2,4096]{3,2,1,0:T(2,128)S(1)}, f32[3,1,2,4096]{3,2,1,0:T(2,128)S(1)}, u32[]{:S(2)}, u32[]{:S(2)}) collective-permute-start(f32[3,1,2,4096]{3,2,1,0:T(2,128)S(1)} %get-tuple-element.36), channel_id=1, source_target_pairs={{1,0},{2,1},{3,2},{4,3},{5,4},{6,5},{7,6},{9,8},{10,9},{11,10},{12... | collective-permute-start | bytes 294920 | tf_op jit(solution)/shard_map/ppermute | solution.py:20
  166.0 7.4 %collective-permute-start.22 = (f32[3,1,2,4096]{3,2,1,0:T(2,128)S(1)}, f32[3,1,2,4096]{3,2,1,0:T(2,128)S(1)}, u32[]{:S(2)}, u32[]{:S(2)}) collective-permute-start(f32[3,1,2,4096]{3,2,1,0:T(2,128)S(1)} %get-tuple-element.35), channel_id=1, source_target_pairs={{0,1},{1,2},{2,3},{3,4},{4,5},{5,6},{6,7},{8,9},{9,10},{10,11},{11... | collective-permute-start | bytes 294920 | tf_op jit(solution)/shard_map/ppermute | solution.py:17
  178.4 5.0 %collective-permute-start.25 = (f32[1,2,2,4096]{3,2,1,0:T(2,128)S(1)}, f32[1,2,2,4096]{3,2,1,0:T(2,128)S(1)}, u32[]{:S(2)}, u32[]{:S(2)}) collective-permute-start(f32[1,2,2,4096]{3,2,1,0:T(2,128)S(1)} %reshape.838), channel_id=1, source_target_pairs={{8,0},{16,8},{24,16},{9,1},{17,9},{25,17},{10,2},{18,10},{26,18},{... | collective-permute-start | bytes 196616 | tf_op jit(solution)/shard_map/ppermute | solution.py:20
  183.4 8.4 %collective-permute-start.27 = (f32[3,1,2,4096]{3,2,1,0:T(2,128)S(1)}, f32[3,1,2,4096]{3,2,1,0:T(2,128)S(1)}, u32[]{:S(2)}, u32[]{:S(2)}) collective-permute-start(f32[3,1,2,4096]{3,2,1,0:T(2,128)S(1)} %get-tuple-element.32), channel_id=1, source_target_pairs={{1,0},{2,1},{3,2},{4,3},{5,4},{6,5},{7,6},{9,8},{10,9},{11,10},{12... | collective-permute-start | bytes 294920 | tf_op jit(solution)/shard_map/ppermute | solution.py:20
  185.4 7.4 %collective-permute-start.26 = (f32[3,1,2,4096]{3,2,1,0:T(2,128)S(1)}, f32[3,1,2,4096]{3,2,1,0:T(2,128)S(1)}, u32[]{:S(2)}, u32[]{:S(2)}) collective-permute-start(f32[3,1,2,4096]{3,2,1,0:T(2,128)S(1)} %get-tuple-element.31), channel_id=1, source_target_pairs={{0,1},{1,2},{2,3},{3,4},{4,5},{5,6},{6,7},{8,9},{9,10},{10,11},{11... | collective-permute-start | bytes 294920 | tf_op jit(solution)/shard_map/ppermute | solution.py:17
  197.7 5.0 %collective-permute-start.29 = (f32[1,2,2,4096]{3,2,1,0:T(2,128)S(1)}, f32[1,2,2,4096]{3,2,1,0:T(2,128)S(1)}, u32[]{:S(2)}, u32[]{:S(2)}) collective-permute-start(f32[1,2,2,4096]{3,2,1,0:T(2,128)S(1)} %reshape.845), channel_id=1, source_target_pairs={{8,0},{16,8},{24,16},{9,1},{17,9},{25,17},{10,2},{18,10},{26,18},{... | collective-permute-start | bytes 196616 | tf_op jit(solution)/shard_map/ppermute | solution.py:20
  202.8 8.2 %collective-permute-start.31 = (f32[3,1,2,4096]{3,2,1,0:T(2,128)S(1)}, f32[3,1,2,4096]{3,2,1,0:T(2,128)S(1)}, u32[]{:S(2)}, u32[]{:S(2)}) collective-permute-start(f32[3,1,2,4096]{3,2,1,0:T(2,128)S(1)} %get-tuple-element.28), channel_id=1, source_target_pairs={{1,0},{2,1},{3,2},{4,3},{5,4},{6,5},{7,6},{9,8},{10,9},{11,10},{12... | collective-permute-start | bytes 294920 | tf_op jit(solution)/shard_map/ppermute | solution.py:20
  204.7 7.4 %collective-permute-start.30 = (f32[3,1,2,4096]{3,2,1,0:T(2,128)S(1)}, f32[3,1,2,4096]{3,2,1,0:T(2,128)S(1)}, u32[]{:S(2)}, u32[]{:S(2)}) collective-permute-start(f32[3,1,2,4096]{3,2,1,0:T(2,128)S(1)} %get-tuple-element.27), channel_id=1, source_target_pairs={{0,1},{1,2},{2,3},{3,4},{4,5},{5,6},{6,7},{8,9},{9,10},{10,11},{11... | collective-permute-start | bytes 294920 | tf_op jit(solution)/shard_map/ppermute | solution.py:17
  217.1 5.0 %collective-permute-start.33 = (f32[1,2,2,4096]{3,2,1,0:T(2,128)S(1)}, f32[1,2,2,4096]{3,2,1,0:T(2,128)S(1)}, u32[]{:S(2)}, u32[]{:S(2)}) collective-permute-start(f32[1,2,2,4096]{3,2,1,0:T(2,128)S(1)} %reshape.852), channel_id=1, source_target_pairs={{8,0},{16,8},{24,16},{9,1},{17,9},{25,17},{10,2},{18,10},{26,18},{... | collective-permute-start | bytes 196616 | tf_op jit(solution)/shard_map/ppermute | solution.py:20
  222.1 8.2 %collective-permute-start.35 = (f32[3,1,2,4096]{3,2,1,0:T(2,128)S(1)}, f32[3,1,2,4096]{3,2,1,0:T(2,128)S(1)}, u32[]{:S(2)}, u32[]{:S(2)}) collective-permute-start(f32[3,1,2,4096]{3,2,1,0:T(2,128)S(1)} %get-tuple-element.24), channel_id=1, source_target_pairs={{1,0},{2,1},{3,2},{4,3},{5,4},{6,5},{7,6},{9,8},{10,9},{11,10},{12... | collective-permute-start | bytes 294920 | tf_op jit(solution)/shard_map/ppermute | solution.py:20
  224.1 7.4 %collective-permute-start.34 = (f32[3,1,2,4096]{3,2,1,0:T(2,128)S(1)}, f32[3,1,2,4096]{3,2,1,0:T(2,128)S(1)}, u32[]{:S(2)}, u32[]{:S(2)}) collective-permute-start(f32[3,1,2,4096]{3,2,1,0:T(2,128)S(1)} %get-tuple-element.23), channel_id=1, source_target_pairs={{0,1},{1,2},{2,3},{3,4},{4,5},{5,6},{6,7},{8,9},{9,10},{10,11},{11... | collective-permute-start | bytes 294920 | tf_op jit(solution)/shard_map/ppermute | solution.py:17
  (7 other events, 60.8 us)
where the time goes:
time: 244 us; the launch traced here: 241 us
  starting transfers between devices  106 us (43%)
  blocking collectives  48.3 us (20%)
  waiting for transfers between devices  35.4 us (15%)
  local copies, waits for them, and re-layouts  21.5 us (9%)
  matrix products  20.5 us (8%)
  other arithmetic  5.01 us (2%)
  between operations  4.02 us (2%)
    ppermute x18, starting transfers between devices, extended(): lax.ppermute(lax.slice_in_dim(block, block.shape[dim] - width, None, axis...  74.2 us
    pmax x1, blocking collectives, local(): lax.pmax(largest_ratio(own_diag, own_off, dof_count), ('slab', 'grp'))  41.7 us
    ppermute x18, starting transfers between devices, extended(): lax.ppermute(lax.slice_in_dim(block, 0, width, axis=dim), axis, backward)  32.2 us
    ppermute x18, waiting for transfers between devices, extended(): lax.ppermute(lax.slice_in_dim(block, 0, width, axis=dim), axis, backward)  26.5 us
    dot_general x56, matrix products, block_apply(): return jnp.einsum('abcij,abcjr->abcir', blocks, vector, precision=highest)  14.5 us
    ppermute x18, waiting for transfers between devices, extended(): lax.ppermute(lax.slice_in_dim(block, block.shape[dim] - width, None, axis...  8.9 us
    another operation x49, local copies, waits for them, and re-layouts  7.18 us
    all_gather x1, blocking collectives, local(): return lax.all_gather(local_flat, 'slab', axis=0, tiled=True)  6.63 us
  transfers between devices with their start and end apart: 36, of which 17 were waited for; matrix products, arithmetic and copies ran while one was open for 6% of the time, Pallas kernels for 0%

commit v1 on v0

v1 whole, which is shorter than its diff:
```python
import jax
import jax.numpy as jnp
from jax import lax
from jax.experimental import pallas as pl
from jax.experimental.pallas import tpu as pltpu
from jax.sharding import PartitionSpec as P

SWEEPS = 8
LANES = 128
FACES = 6
PADM = 32
GROUPS = 4

f32 = jnp.float32
bf16 = jnp.bfloat16


def halves(x):
    hi = x.astype(bf16)
    lo = (x - hi.astype(f32)).astype(bf16)
    return hi, lo


def contract0(a, b):
    return lax.dot_general(a, b, (((0,), (0,)), ((), ())), preferred_element_type=f32)


def coarse_kernel(slot_s, dens, slot_v, links, code, prolong, rhs, out, pairs, info):
    kids, dof, _ = prolong.shape
    half = dof // 2
    _, rows_b, rows_c, _ = dens.shape
    count = rows_b * rows_c
    groups = rhs.shape[2] // 4
    for s in range(kids):
        even = prolong[s, pl.ds(0, half, stride=2), :]
        odd = prolong[s, pl.ds(1, half, stride=2), :]
        hi, lo = halves(jnp.concatenate([even, odd], axis=1))
        pairs[s] = jnp.concatenate([hi, lo], axis=1)
    info[...] = jnp.zeros(info.shape, f32)
    for a in range(count):
        b, c = a // rows_c, a % rows_c
        info[a : a + 1, 0:kids] = dens[0, b, c : c + 1, :]
        info[a : a + 1, kids : 2 * kids] = slot_v[0, b, c : c + 1, :].astype(f32)
        info[a : a + 1, 2 * kids : 2 * kids + FACES] = jnp.where(
            links[0, b, c : c + 1, :] >= 0, f32(1.0), f32(0.0)
        )
        info[a : a + 1, 3 * kids : 3 * kids + FACES] = code[0, b, c : c + 1, :].astype(f32)
    members = out.shape[0]
    for a in range(count):
        b, c = a // rows_c, a % rows_c
        weights = jnp.concatenate([pairs[slot_s[0, b, c, q]] for q in range(kids)], axis=0)
        prod = contract0(rhs[a], weights)
        prod = prod[:, :LANES] + prod[:, LANES:]
        own = prod[:dof, :dof] + prod[dof:, dof:]
        row = jnp.concatenate([own[:groups], own[groups:]], axis=1)
        for first in range(0, members, groups):
            out[first : first + groups, a, :] = row
    out[:, count : 2 * count, :] = jnp.broadcast_to(info[0:count, :][None], (members, count, LANES))


def matrices_kernel(stiffness, prolong, penalty, stacked, columns, mall, extra):
    kids, dof, _ = prolong.shape
    codes = penalty.shape[0]
    s_hi, s_lo = halves(stiffness[...])
    s_left = jnp.concatenate([s_hi, s_hi, s_lo], axis=1)
    for s in range(kids):
        p_hi, p_lo = halves(prolong[s])
        sp = jnp.dot(s_left, jnp.concatenate([p_hi, p_lo, p_hi], axis=0), preferred_element_type=f32)
        q_hi, q_lo = halves(sp)
        mall[s] = contract0(
            jnp.concatenate([p_hi, p_hi, p_lo], axis=0), jnp.concatenate([q_hi, q_lo, q_hi], axis=0)
        )
    mall[kids : kids + codes] = penalty[...]
    mall[kids + codes :] = jnp.zeros((PADM - kids - codes, dof, dof), f32)
    rows = dof // GROUPS
    eye = (
        lax.broadcasted_iota(jnp.int32, (dof, dof), 0) == lax.broadcasted_iota(jnp.int32, (dof, dof), 1)
    ).astype(f32)
    extra[...] = jnp.zeros(extra.shape, f32)
    for m in range(kids + codes):
        mat = mall[m]
        hi, lo = halves(mat)
        wide = jnp.concatenate([hi, hi, lo], axis=1)
        for g in range(GROUPS):
            stacked[g, m * rows : (m + 1) * rows, :] = wide[g * rows : (g + 1) * rows]
        extra[m : m + 1, 0:dof] = jnp.sum(mat * eye, axis=0, keepdims=True)
        if m >= kids:
            extra[m : m + 1, dof : 2 * dof] = jnp.sum(jnp.abs(mat), axis=0, keepdims=True)
    for pair in range(dof // 2 + 1):
        if pair < dof // 2:
            both = jnp.concatenate([mall[:, 2 * pair, :], mall[:, 2 * pair + 1, :]], axis=1)
        else:
            both = extra[...]
        hi, lo = halves(both.T)
        columns[pair] = jnp.concatenate([hi, hi, lo], axis=1)


def solve_kernel(strides, got, stacked, columns, out, flat, resid, update, answer, coefs, tiles):
    count = got.shape[1] // 2
    members = got.shape[0]
    total = members * count
    dof = resid.shape[0]
    kids = 8
    rows = dof // GROUPS
    for a in range(count):
        flat[0, pl.ds(a, members, stride=count), :] = got[:, a, :]
        flat[1, pl.ds(a, members, stride=count), :] = got[:, count + a, :]
    coarse = flat[0].T
    facts = flat[1].T
    dens = facts[0:kids]
    slots = facts[kids : 2 * kids]
    open_face = facts[2 * kids : 2 * kids + FACES] > 0.5
    codes = facts[3 * kids : 3 * kids + FACES].astype(jnp.int32)
    rho = jnp.sum(dens, axis=0, keepdims=True) * f32(1.0 / kids)
    inverse = 1.0 / dens
    place = lax.broadcasted_iota(jnp.int32, (kids, total), 0).astype(f32)
    weight = jnp.zeros((kids, total), f32)
    for q in range(kids):
        weight = weight + jnp.where(slots[q : q + 1] == place, inverse[q : q + 1], 0.0)
    shifts = [sign * stride for stride in strides for sign in (-1, 1)]
    code_place = lax.broadcasted_iota(jnp.int32, (16, total), 0)
    face_sum = jnp.zeros((16, total), f32)
    face_w = []
    for f in range(FACES):
        other = pltpu.roll(rho, (-shifts[f]) % total, 1)
        fw = jnp.where(open_face[f : f + 1], 2.0 / (rho + other), 0.0)
        face_w.append(fw)
        face_sum = face_sum + jnp.where(codes[f : f + 1] == code_place, fw, 0.0)
    coef = jnp.concatenate([weight, face_sum, jnp.zeros((8, total), f32)], axis=0)
    c_hi, c_lo = halves(coef)
    c_all = jnp.concatenate([c_hi, c_lo, c_hi], axis=0)
    last = jnp.dot(columns[dof // 2], c_all, preferred_element_type=f32)
    jacobi = last[:dof]
    sums = last[dof:]
    for pair in range(dof // 2):
        part = jnp.abs(jnp.dot(columns[pair], c_all, preferred_element_type=f32))
        sums = sums + (part[:dof] + part[dof:])
    upper = jnp.max(jnp.max(sums / jacobi, axis=0, keepdims=True), axis=1, keepdims=True)
    lower = upper / 10.0
    centre = 0.5 * (upper + lower)
    half_width = 0.5 * (upper - lower)
    sigma = centre / half_width
    damping = 1.0 / sigma
    inv_jac = 1.0 / jacobi
    inv_jac = jnp.concatenate([inv_jac, inv_jac], axis=1)
    start = jnp.concatenate([coarse[:dof], coarse[dof:]], axis=1)
    resid[...] = start
    start = start * inv_jac / centre
    update[...] = start
    answer[...] = start
    for f in range(FACES):
        coefs[f : f + 1, :] = jnp.concatenate([face_w[f], face_w[f]], axis=1)
        fc = codes[f : f + 1].astype(f32)
        coefs[8 + f : 9 + f, :] = jnp.concatenate([fc, fc], axis=1)
    coefs[16:24, :] = jnp.concatenate([weight, weight], axis=1)
    jac2 = inv_jac

    def sweep(_, damp):
        hi, lo = halves(update[...])
        right = jnp.concatenate([hi, lo, hi], axis=0)
        damp_next = 1.0 / (2.0 * sigma - damp)
        keep = damp_next * damp
        gain = 2.0 * damp_next / half_width
        for g in range(GROUPS):
            prod = jnp.dot(stacked[g], right, preferred_element_type=f32)
            mats = [prod[m * rows : (m + 1) * rows] for m in range(24)]
            applied = coefs[16:17] * mats[0]
            for s in range(1, kids):
                applied = applied + coefs[16 + s : 17 + s] * mats[s]
            terms = []
            for f in range(FACES):
                fc = coefs[8 + f : 9 + f].astype(jnp.int32)
                fc = jnp.broadcast_to(fc, (rows, 2 * total))
                level = mats[kids:]
                for bit in range(4):
                    on = ((fc >> bit) & 1) > 0
                    level = [
                        jnp.where(on, level[2 * n + 1], level[2 * n]) for n in range(len(level) // 2)
                    ]
                terms.append(coefs[f : f + 1] * level[0])
            for f in range(FACES):
                moved = terms[f ^ 1]
                moved = jnp.concatenate(
                    [
                        pltpu.roll(moved[:, :total], (-shifts[f]) % total, 1),
                        pltpu.roll(moved[:, total:], (-shifts[f]) % total, 1),
                    ],
                    axis=1,
                )
                applied = applied + (terms[f] - moved)
            part = pl.ds(g * rows, rows)
            left = resid[part, :] - applied
            resid[part, :] = left
            new = keep * update[part, :] + gain * (left * jac2[g * rows : (g + 1) * rows])
            update[part, :] = new
            answer[part, :] = answer[part, :] + new
        return damp_next

    lax.fori_loop(0, SWEEPS, sweep, damping)
    grp_count = strides[0] // count
    firsts = total // strides[0]
    half = dof // 2
    lane_tiles = total // LANES
    for t in range(2 * lane_tiles):
        tiles[t] = answer[:, t * LANES : (t + 1) * LANES]
    for low in range(2):
        for c in range(2):
            for t in range(lane_tiles):
                block = tiles[c * lane_tiles + t, pl.ds(low, half, stride=2), :]
                flat[0, t * LANES : (t + 1) * LANES, 0:half] = block.T
            row = jnp.concatenate(
                [flat[0, pl.ds(n, members, stride=count), 0:half] for n in range(count)], axis=1
            )
            for i in range(firsts):
                piece = row[i * grp_count : (i + 1) * grp_count]
                for s in range(members // grp_count):
                    out[pl.ds(s * grp_count, grp_count), (low * 2 + c) * firsts + i, :] = piece


def finish_kernel(got, out):
    firsts = got.shape[1] // 4
    sources = 32
    rows_b, rows_c = 2, 2
    half = 32
    for i in range(firsts):
        block = jnp.concatenate([got[0:sources, x * firsts + i, :] for x in range(4)], axis=0).T
        for n in range(rows_b * rows_c):
            b, c = n // rows_c, n % rows_c
            out[i * rows_b + b, pl.ds(c, half, stride=rows_c), :] = block[n * half : (n + 1) * half]


def vmem():
    return pl.BlockSpec(memory_space=pltpu.VMEM)


def local(cell_density, cell_slot, neighbours, face_code, stiffness, prolong, penalty, fine_rhs):
    _, rows_b, rows_c, kids = cell_density.shape
    dof = stiffness.shape[0]
    count = rows_b * rows_c
    slabs, grps = lax.axis_size("slab"), lax.axis_size("grp")
    members = slabs * grps
    total = members * count
    every = ("slab", "grp")
    strides = (grps * count, rows_c, 1)
    rhs = fine_rhs.reshape(count, kids * dof // 2, LANES)
    sent = pl.pallas_call(
        coarse_kernel,
        out_shape=jax.ShapeDtypeStruct((members, 2 * count, LANES), f32),
        in_specs=[pl.BlockSpec(memory_space=pltpu.SMEM)] + [vmem()] * 6,
        out_specs=vmem(),
        scratch_shapes=[pltpu.VMEM((kids, dof // 2, 2 * LANES), bf16), pltpu.VMEM((8, LANES), f32)],
        name="coarse",
    )(cell_slot, cell_density, cell_slot, neighbours, face_code, prolong, rhs)
    got = lax.all_to_all(sent, every, 0, 0, tiled=True)
    stacked, columns = pl.pallas_call(
        matrices_kernel,
        out_shape=(
            jax.ShapeDtypeStruct((GROUPS, 24 * (dof // GROUPS), 3 * dof), bf16),
            jax.ShapeDtypeStruct((dof // 2 + 1, 2 * dof, 3 * PADM), bf16),
        ),
        in_specs=[vmem()] * 3,
        out_specs=(vmem(), vmem()),
        scratch_shapes=[pltpu.VMEM((PADM, dof, dof), f32), pltpu.VMEM((PADM, 2 * dof), f32)],
        name="matrices",
    )(stiffness, prolong, penalty)
    back = pl.pallas_call(
        lambda *refs: solve_kernel(strides, *refs),
        out_shape=jax.ShapeDtypeStruct((members, 4 * slabs, LANES), f32),
        in_specs=[vmem()] * 3,
        out_specs=vmem(),
        scratch_shapes=[
            pltpu.VMEM((2, total, LANES), f32),
            pltpu.VMEM((dof, 2 * total), f32),
            pltpu.VMEM((dof, 2 * total), f32),
            pltpu.VMEM((dof, 2 * total), f32),
            pltpu.VMEM((24, 2 * total), f32),
            pltpu.VMEM((2 * total // LANES, dof, LANES), f32),
        ],
        name="solve",
    )(got, stacked, columns)
    back = lax.all_to_all(back, every, 0, 0, tiled=True)
    full = pl.pallas_call(
        finish_kernel,
        out_shape=jax.ShapeDtypeStruct((slabs * rows_b, dof, LANES), f32),
        in_specs=[vmem()],
        out_specs=vmem(),
        name="finish",
    )(back)
    full = full.reshape(slabs, rows_b, dof // 2, rows_c, LANES).transpose(0, 1, 3, 2, 4)
    return full.reshape(slabs, rows_b, rows_c, dof // 2 * LANES)


def solution(mesh):
    return jax.shard_map(
        local,
        mesh=mesh,
        in_specs=(
            P("slab", "grp", None, None),
            P("slab", "grp", None, None),
            P("slab", "grp", None, None),
            P("slab", "grp", None, None),
            P(),
            P(),
            P(),
            P("slab", "grp", None, None, None),
        ),
        out_specs=P(None, "grp", None, None),
        check_vma=False,
    )
```

time: 244 us -> 46.4 us (0.19)
  starting transfers between devices: 106 us -> 7.08 us
  waiting for transfers between devices: 35.4 us -> 0.47 us
  blocking collectives: 48.3 us -> 16 us
  matrix products: 20.5 us -> 0 us
  Pallas kernels: 0 us -> 20.1 us
  local copies, waits for them, and re-layouts: 21.5 us -> 2.43 us
  other arithmetic: 5.01 us -> 0 us
  between operations: 4.02 us -> 0.01 us
    ppermute x36 -> x0, starting transfers between devices: 106 us -> none  [the longest x18 74.2 us: extended(): lax.ppermute(lax.slice_in_dim(block, block.shape[dim] - width, None, axis...]
    pmax x1 -> x0, blocking collectives: 41.7 us -> none  [local(): lax.pmax(largest_ratio(own_diag, own_off, dof_count), ('slab', 'grp'))]
    ppermute x36 -> x0, waiting for transfers between devices: 35.4 us -> none  [the longest x18 26.5 us: extended(): lax.ppermute(lax.slice_in_dim(block, 0, width, axis=dim), axis, backward)]
    dot_general x64 -> x0, matrix products: 20.5 us -> none  [the longest x56 14.5 us: block_apply(): return jnp.einsum('abcij,abcjr->abcir', blocks, vector, precision=highest)]
    pallas_call x0 -> x4, Pallas kernels: none -> 20.1 us  [the longest x1 8.24 us: local(): pl.pallas_call(lambda *refs: solve_kernel(strides, *refs), out_shape=jax....]
    all_to_all x0 -> x1, blocking collectives: none -> 16 us  [local(): back = lax.all_to_all(back, every, 0, 0, tiled=True)]
    another operation x59 -> x0, local copies, waits for them, and re-layouts: 12.8 us -> none
    all_to_all x0 -> x1, starting transfers between devices: none -> 7.08 us  [local(): got = lax.all_to_all(sent, every, 0, 0, tiled=True)]
  transfers between devices with their start and end apart: 36 -> 1, of which waited for: 17 -> 1; matrix products, arithmetic and copies ran while one was open for 6% -> 0% of each run, Pallas kernels for 0% -> 17%
where the time goes in v1:
time: 46.4 us; the launch traced here: 46 us
  Pallas kernels  20.1 us (43%)
  blocking collectives  16 us (34%)
  starting transfers between devices  7.08 us (15%)
  local copies, waits for them, and re-layouts  2.43 us (5%)
  waiting for transfers between devices  0.47 us (1%)
    all_to_all x1, blocking collectives, local(): back = lax.all_to_all(back, every, 0, 0, tiled=True)  16 us
    pallas_call x1, Pallas kernels, local(): pl.pallas_call(lambda *refs: solve_kernel(strides, *refs), out_shape=jax....  8.24 us
    pallas_call x1, Pallas kernels, local(): pl.pallas_call(matrices_kernel, out_shape=(jax.ShapeDtypeStruct((GROUPS,...  7.74 us
    all_to_all x1, starting transfers between devices, local(): got = lax.all_to_all(sent, every, 0, 0, tiled=True)  7.08 us
    pallas_call x1, Pallas kernels, local(): pl.pallas_call(coarse_kernel, out_shape=jax.ShapeDtypeStruct((members, 2...  2.25 us
    pallas_call x1, Pallas kernels, local(): pl.pallas_call(finish_kernel, out_shape=jax.ShapeDtypeStruct((slabs * row...  1.86 us
    reshape x1, local copies, waits for them, and re-layouts, local(): rhs = fine_rhs.reshape(count, kids * dof // 2, LANES)  1.77 us
  transfers between devices with their start and end apart: 1, of which 1 were waited for; matrix products, arithmetic and copies ran while one was open for 0% of the time, Pallas kernels for 17%

profile of v1, /device:TPU:1, one launch (start us, length us, event | category | flops | bytes accessed | tf_op | source)
XLA Modules:
  0.0 46.0 jit_solution(15525024390101754868)
XLA Ops:
  0.0 1.8 %reshape.9.rhs = bf16[4,256,128]{2,1,0:T(8,128)(2,1)} reshape(bf16[1,2,2,8,4096]{4,3,2,1,0:T(8,128)(2,1)} %param.15) | data formatting | bytes 524288 | tf_op jit(solution)/shard_map/reshape | solution.py:245
  1.8 2.3 %coarse.1 = f32[32,8,128]{2,1,0:T(8,128)} custom-call(s32[1,2,2,8]{3,2,1,0:T(2,128)} %slot_v.1, f32[1,2,2,8]{3,2,1,0:T(2,128)} %dens.1, s32[1,2,2,8]{3,2,1,0:T(2,128)} %slot_v.1, s32[1,2,2,6]{3,2,1,0:T(2,128)} %links.1, s32[1,2,2,6]{3,2,1,0:T(2,128)} %code.1, f32[8,64,64]{2,1,0:T(8,128)} %prolong.3, bf16[4,256,128]{2,1,0:T(8,128)(2,1)} %reshape.9.rhs), custom_call_target="tpu_custom_call" | custom-call | tf_op jit(solution)/shard_map/coarse/pallas_call | solution.py:246
  4.0 7.1 %all-to-all-start = ((f32[32,8,128]{2,1,0:T(8,128)}), f32[32,8,128]{2,1,0:T(8,128)S(1)}, u32[]{:S(2)}, u32[]{:S(2)}) async-start(f32[32,8,128]{2,1,0:T(8,128)} %coarse.1), calls=%async_computation | async-start | bytes 262144 | tf_op jit(solution)/shard_map/all_to_all | solution.py:254
  11.1 7.7 %matrices.1 = (bf16[4,384,192]{2,1,0:T(8,128)(2,1)}, bf16[33,128,96]{2,1,0:T(8,128)(2,1)}) custom-call(f32[64,64]{1,0:T(8,128)} %stiffness.1, f32[8,64,64]{2,1,0:T(8,128)} %prolong.3, f32[16,64,64]{2,1,0:T(8,128)} %penalty.1), custom_call_target="tpu_custom_call" | custom-call | tf_op jit(solution)/shard_map/matrices/pallas_call | solution.py:255
  18.9 0.5 %all-to-all-done.refs_0_ = f32[32,8,128]{2,1,0:T(8,128)S(1)} async-done(((f32[32,8,128]{2,1,0:T(8,128)}), f32[32,8,128]{2,1,0:T(8,128)S(1)}, u32[]{:S(2)}, u32[]{:S(2)}) %all-to-all-start) | async-done | bytes 131104 | tf_op jit(solution)/shard_map/all_to_all | solution.py:254
  19.3 0.0 copy-start
  19.3 0.7 %copy-done = f32[32,8,128]{2,1,0:T(8,128)} copy-done((f32[32,8,128]{2,1,0:T(8,128)}, f32[32,8,128]{2,1,0:T(8,128)S(1)}, u32[]{:S(2)}) %copy-start) | copy-done | bytes 131096
  20.0 8.2 %solve.1 = f32[32,16,128]{2,1,0:T(8,128)} custom-call(f32[32,8,128]{2,1,0:T(8,128)} %copy-done, bf16[4,384,192]{2,1,0:T(8,128)(2,1)} %get-tuple-element.7.refs_1_, bf16[33,128,96]{2,1,0:T(8,128)(2,1)} %get-tuple-element.8.refs_2_), custom_call_target="tpu_custom_call" | custom-call | tf_op jit(solution)/shard_map/solve/pallas_call | solution.py:266
  28.2 16.0 %all_to_all.10.got = f32[32,16,128]{2,1,0:T(8,128)} all-to-all(f32[32,16,128]{2,1,0:T(8,128)} %solve.1), channel_id=1, replica_groups=mesh['slab'=4,'grp'=8] {'slab','grp'}, dimensions={0} | all-to-all | bytes 524288 | tf_op jit(solution)/shard_map/all_to_all | solution.py:281
  44.2 1.9 %finish.1 = f32[8,64,128]{2,1,0:T(8,128)} custom-call(f32[32,16,128]{2,1,0:T(8,128)} %all_to_all.10.got), custom_call_target="tpu_custom_call" | custom-call | tf_op jit(solution)/shard_map/finish/pallas_call | solution.py:282
Async XLA Ops:
  4.0 15.3 %all-to-all-start = ((f32[32,8,128]{2,1,0:T(8,128)}), f32[32,8,128]{2,1,0:T(8,128)S(1)}, u32[]{:S(2)}, u32[]{:S(2)}) async-start(f32[32,8,128]{2,1,0:T(8,128)} %coarse.1), calls=%async_computation | async-start | bytes 262144 | tf_op jit(solution)/shard_map/all_to_all | solution.py:254
  19.3 0.7 %copy-start = (f32[32,8,128]{2,1,0:T(8,128)}, f32[32,8,128]{2,1,0:T(8,128)S(1)}, u32[]{:S(2)}) copy-start(f32[32,8,128]{2,1,0:T(8,128)S(1)} %all-to-all-done.refs_0_) | copy-start | bytes 393220

commit v2 on v1

--- a/solution.py
+++ b/solution.py
@@ -25,17 +25,13 @@
     return lax.dot_general(a, b, (((0,), (0,)), ((), ())), preferred_element_type=f32)
 
 
-def coarse_kernel(slot_s, dens, slot_v, links, code, prolong, rhs, out, pairs, info):
+def coarse_kernel(slot_s, dens, slot_v, links, code, prolong, rhs, out, wide, pairs, weights, info):
     kids, dof, _ = prolong.shape
     half = dof // 2
     _, rows_b, rows_c, _ = dens.shape
     count = rows_b * rows_c
-    groups = rhs.shape[2] // 4
-    for s in range(kids):
-        even = prolong[s, pl.ds(0, half, stride=2), :]
-        odd = prolong[s, pl.ds(1, half, stride=2), :]
-        hi, lo = halves(jnp.concatenate([even, odd], axis=1))
-        pairs[s] = jnp.concatenate([hi, lo], axis=1)
+    members = out.shape[0]
+    groups = half
     info[...] = jnp.zeros(info.shape, f32)
     for a in range(count):
         b, c = a // rows_c, a % rows_c
@@ -45,54 +41,63 @@
             links[0, b, c : c + 1, :] >= 0, f32(1.0), f32(0.0)
         )
         info[a : a + 1, 3 * kids : 3 * kids + FACES] = code[0, b, c : c + 1, :].astype(f32)
-    members = out.shape[0]
+    out[:, count : 2 * count, :] = jnp.broadcast_to(info[0:count, :][None], (members, count, LANES))
+    first_half = lax.broadcasted_iota(jnp.int32, (half, LANES), 1) < dof
+    for s in range(kids):
+        wide[s, :, 0:dof] = prolong[s]
+        even = wide[s, pl.ds(0, half, stride=2), :]
+        odd = wide[s, pl.ds(1, half, stride=2), :]
+        pairs[s] = jnp.where(first_half, even, pltpu.roll(odd, dof, 1))
     for a in range(count):
         b, c = a // rows_c, a % rows_c
-        weights = jnp.concatenate([pairs[slot_s[0, b, c, q]] for q in range(kids)], axis=0)
-        prod = contract0(rhs[a], weights)
+        for q in range(kids):
+            weights[a, pl.ds(q, half, stride=kids), :] = pairs[slot_s[0, b, c, q]]
+    for a in range(count):
+        b, c = a // rows_c, a % rows_c
+        cells = rhs[0, b, c].astype(f32)
+        cells = jnp.concatenate([cells[:, t * LANES : (t + 1) * LANES] for t in range(half)], axis=0)
+        hi, lo = halves(weights[a])
+        prod = contract0(cells.astype(bf16), jnp.concatenate([hi, lo], axis=1))
         prod = prod[:, :LANES] + prod[:, LANES:]
         own = prod[:dof, :dof] + prod[dof:, dof:]
         row = jnp.concatenate([own[:groups], own[groups:]], axis=1)
         for first in range(0, members, groups):
             out[first : first + groups, a, :] = row
-    out[:, count : 2 * count, :] = jnp.broadcast_to(info[0:count, :][None], (members, count, LANES))
 
 
 def matrices_kernel(stiffness, prolong, penalty, stacked, columns, mall, extra):
     kids, dof, _ = prolong.shape
     codes = penalty.shape[0]
+    half = dof // 2
+    rows = dof // GROUPS
     s_hi, s_lo = halves(stiffness[...])
     s_left = jnp.concatenate([s_hi, s_hi, s_lo], axis=1)
-    for s in range(kids):
-        p_hi, p_lo = halves(prolong[s])
-        sp = jnp.dot(s_left, jnp.concatenate([p_hi, p_lo, p_hi], axis=0), preferred_element_type=f32)
-        q_hi, q_lo = halves(sp)
-        mall[s] = contract0(
-            jnp.concatenate([p_hi, p_hi, p_lo], axis=0), jnp.concatenate([q_hi, q_lo, q_hi], axis=0)
-        )
-    mall[kids : kids + codes] = penalty[...]
-    mall[kids + codes :] = jnp.zeros((PADM - kids - codes, dof, dof), f32)
-    rows = dof // GROUPS
     eye = (
         lax.broadcasted_iota(jnp.int32, (dof, dof), 0) == lax.broadcasted_iota(jnp.int32, (dof, dof), 1)
     ).astype(f32)
     extra[...] = jnp.zeros(extra.shape, f32)
+    mall[kids + codes :] = jnp.zeros((PADM - kids - codes, half, 2 * dof), f32)
     for m in range(kids + codes):
-        mat = mall[m]
+        if m < kids:
+            p_hi, p_lo = halves(prolong[m])
+            right = jnp.concatenate([p_hi, p_lo, p_hi], axis=0)
+            q_hi, q_lo = halves(jnp.dot(s_left, right, preferred_element_type=f32))
+            mat = contract0(
+                jnp.concatenate([p_hi, p_hi, p_lo], axis=0), jnp.concatenate([q_hi, q_lo, q_hi], axis=0)
+            )
+        else:
+            mat = penalty[m - kids]
+            extra[m : m + 1, dof : 2 * dof] = jnp.sum(jnp.abs(mat), axis=0, keepdims=True)
+        extra[m : m + 1, 0:dof] = jnp.sum(mat * eye, axis=0, keepdims=True)
+        mall[m, :, 0:dof] = mat[:half]
+        mall[m, :, dof : 2 * dof] = mat[half:]
         hi, lo = halves(mat)
         wide = jnp.concatenate([hi, hi, lo], axis=1)
         for g in range(GROUPS):
             stacked[g, m * rows : (m + 1) * rows, :] = wide[g * rows : (g + 1) * rows]
-        extra[m : m + 1, 0:dof] = jnp.sum(mat * eye, axis=0, keepdims=True)
-        if m >= kids:
-            extra[m : m + 1, dof : 2 * dof] = jnp.sum(jnp.abs(mat), axis=0, keepdims=True)
-    for pair in range(dof // 2 + 1):
-        if pair < dof // 2:
-            both = jnp.concatenate([mall[:, 2 * pair, :], mall[:, 2 * pair + 1, :]], axis=1)
-        else:
-            both = extra[...]
-        hi, lo = halves(both.T)
-        columns[pair] = jnp.concatenate([hi, hi, lo], axis=1)
+    for pair in range(half + 1):
+        hi, lo = halves(mall[:, pair, :] if pair < half else extra[...])
+        columns[pair] = jnp.concatenate([hi, hi, lo], axis=0).T
 
 
 def solve_kernel(strides, got, stacked, columns, out, flat, resid, update, answer, coefs, tiles):
@@ -233,6 +238,10 @@
     return pl.BlockSpec(memory_space=pltpu.VMEM)
 
 
+def near(x):
+    return pltpu.with_memory_space_constraint(x, pltpu.VMEM)
+
+
 def local(cell_density, cell_slot, neighbours, face_code, stiffness, prolong, penalty, fine_rhs):
     _, rows_b, rows_c, kids = cell_density.shape
     dof = stiffness.shape[0]
@@ -242,30 +251,35 @@
     total = members * count
     every = ("slab", "grp")
     strides = (grps * count, rows_c, 1)
-    rhs = fine_rhs.reshape(count, kids * dof // 2, LANES)
     sent = pl.pallas_call(
         coarse_kernel,
-        out_shape=jax.ShapeDtypeStruct((members, 2 * count, LANES), f32),
+        out_shape=pltpu.VMEM((members, 2 * count, LANES), f32),
         in_specs=[pl.BlockSpec(memory_space=pltpu.SMEM)] + [vmem()] * 6,
         out_specs=vmem(),
-        scratch_shapes=[pltpu.VMEM((kids, dof // 2, 2 * LANES), bf16), pltpu.VMEM((8, LANES), f32)],
+        scratch_shapes=[
+            pltpu.VMEM((kids, dof, LANES), f32),
+            pltpu.VMEM((kids, dof // 2, LANES), f32),
+            pltpu.VMEM((count, kids * dof // 2, LANES), f32),
+            pltpu.VMEM((8, LANES), f32),
+        ],
         name="coarse",
-    )(cell_slot, cell_density, cell_slot, neighbours, face_code, prolong, rhs)
+    )(cell_slot, cell_density, cell_slot, neighbours, face_code, prolong, fine_rhs)
     got = lax.all_to_all(sent, every, 0, 0, tiled=True)
     stacked, columns = pl.pallas_call(
         matrices_kernel,
         out_shape=(
-            jax.ShapeDtypeStruct((GROUPS, 24 * (dof // GROUPS), 3 * dof), bf16),
-            jax.ShapeDtypeStruct((dof // 2 + 1, 2 * dof, 3 * PADM), bf16),
+            pltpu.VMEM((GROUPS, 24 * (dof // GROUPS), 3 * dof), bf16),
+            pltpu.VMEM((dof // 2 + 1, 2 * dof, 3 * PADM), bf16),
         ),
         in_specs=[vmem()] * 3,
         out_specs=(vmem(), vmem()),
-        scratch_shapes=[pltpu.VMEM((PADM, dof, dof), f32), pltpu.VMEM((PADM, 2 * dof), f32)],
+        scratch_shapes=[pltpu.VMEM((PADM, dof // 2, 2 * dof), f32), pltpu.VMEM((PADM, 2 * dof), f32)],
+        compiler_params=pltpu.CompilerParams(vmem_limit_bytes=24 << 20),
         name="matrices",
-    )(stiffness, prolong, penalty)
+    )(near(stiffness), near(prolong), near(penalty))
     back = pl.pallas_call(
         lambda *refs: solve_kernel(strides, *refs),
-        out_shape=jax.ShapeDtypeStruct((members, 4 * slabs, LANES), f32),
+        out_shape=pltpu.VMEM((members, 4 * slabs, LANES), f32),
         in_specs=[vmem()] * 3,
         out_specs=vmem(),
         scratch_shapes=[
@@ -276,16 +290,18 @@
             pltpu.VMEM((24, 2 * total), f32),
             pltpu.VMEM((2 * total // LANES, dof, LANES), f32),
         ],
+        compiler_params=pltpu.CompilerParams(vmem_limit_bytes=40 << 20),
         name="solve",
-    )(got, stacked, columns)
+    )(near(got), near(stacked), near(columns))
     back = lax.all_to_all(back, every, 0, 0, tiled=True)
     full = pl.pallas_call(
         finish_kernel,
         out_shape=jax.ShapeDtypeStruct((slabs * rows_b, dof, LANES), f32),
         in_specs=[vmem()],
         out_specs=vmem(),
+        compiler_params=pltpu.CompilerParams(vmem_limit_bytes=24 << 20),
         name="finish",
-    )(back)
+    )(near(back))
     full = full.reshape(slabs, rows_b, dof // 2, rows_c, LANES).transpose(0, 1, 3, 2, 4)
     return full.reshape(slabs, rows_b, rows_c, dof // 2 * LANES)
 

time: 46.4 us -> 37 us (0.80)
  Pallas kernels: 20.1 us -> 11.2 us
  waiting for transfers between devices: 0.47 us -> 5.47 us
  blocking collectives: 16 us -> 12.2 us
  local copies, waits for them, and re-layouts: 2.43 us -> 0.76 us
    pallas_call x3, Pallas kernels: 18.2 us -> 10.3 us  [the longest x1 5.98 us: local(): pl.pallas_call(lambda *refs: solve_kernel(strides, *refs), out_shape=pltp...]
    all_to_all x1, waiting for transfers between devices: 0.47 us -> 5.47 us  [local(): got = lax.all_to_all(sent, every, 0, 0, tiled=True)]
    all_to_all x1, blocking collectives: 16 us -> 12.2 us  [local(): back = lax.all_to_all(back, every, 0, 0, tiled=True)]
    reshape x1 -> x0, local copies, waits for them, and re-layouts: 1.77 us -> none  [local(): rhs = fine_rhs.reshape(count, kids * dof // 2, LANES)]
    pallas_call x1, Pallas kernels: 1.86 us -> 0.91 us  [local(): pl.pallas_call(finish_kernel, out_shape=jax.ShapeDtypeStruct((slabs * row...]
  transfers between devices with their start and end apart: 1 -> 1, of which waited for: 1 -> 1; matrix products, arithmetic and copies ran while one was open for 0% -> 0% of each run, Pallas kernels for 17% -> 5%
where the time goes in v2:
time: 37 us; the launch traced here: 36.7 us
  blocking collectives  12.2 us (33%)
  Pallas kernels  11.2 us (30%)
  starting transfers between devices  7.08 us (19%)
  waiting for transfers between devices  5.47 us (15%)
  local copies, waits for them, and re-layouts  0.76 us (2%)
    all_to_all x1, blocking collectives, local(): back = lax.all_to_all(back, every, 0, 0, tiled=True)  12.2 us
    all_to_all x1, starting transfers between devices, local(): got = lax.all_to_all(sent, every, 0, 0, tiled=True)  7.08 us
    pallas_call x1, Pallas kernels, local(): pl.pallas_call(lambda *refs: solve_kernel(strides, *refs), out_shape=pltp...  5.98 us
    all_to_all x1, waiting for transfers between devices, local(): got = lax.all_to_all(sent, every, 0, 0, tiled=True)  5.47 us
    pallas_call x1, Pallas kernels, local(): pl.pallas_call(coarse_kernel, out_shape=pltpu.VMEM((members, 2 * count, L...  2.38 us
    pallas_call x1, Pallas kernels, local(): pl.pallas_call(matrices_kernel, out_shape=(pltpu.VMEM((GROUPS, 24 * (dof...  1.95 us
    pallas_call x1, Pallas kernels, local(): pl.pallas_call(finish_kernel, out_shape=jax.ShapeDtypeStruct((slabs * row...  0.91 us
    unnamed x6, local copies, waits for them, and re-layouts  0.76 us
  transfers between devices with their start and end apart: 1, of which 1 were waited for; matrix products, arithmetic and copies ran while one was open for 0% of the time, Pallas kernels for 5%

profile of v2, /device:TPU:1, one launch (start us, length us, event | category | flops | bytes accessed | tf_op | source)
XLA Modules:
  0.0 36.7 jit_solution(7352612714661780906)
XLA Ops:
  0.0 0.0 copy-start
  0.0 0.0 copy-start.1
  0.0 2.4 %coarse.1 = f32[32,8,128]{2,1,0:T(8,128)} custom-call(s32[1,2,2,8]{3,2,1,0:T(2,128)} %slot_v.1, f32[1,2,2,8]{3,2,1,0:T(2,128)} %dens.1, s32[1,2,2,8]{3,2,1,0:T(2,128)} %slot_v.1, s32[1,2,2,6]{3,2,1,0:T(2,128)} %links.1, s32[1,2,2,6]{3,2,1,0:T(2,128)} %code.1, f32[8,64,64]{2,1,0:T(8,128)} %prolong.3, bf16[1,2,2,8,4096]{4,3,2,1,0:T(8,128)(2,1)} %rhs.1), custom_call_target="tpu_custom_call" | custom-call | tf_op jit(solution)/shard_map/coarse/pallas_call | solution.py:254
  2.4 7.1 %all-to-all-start = ((f32[32,8,128]{2,1,0:T(8,128)}), f32[32,8,128]{2,1,0:T(8,128)S(1)}, u32[]{:S(2)}, u32[]{:S(2)}) async-start(f32[32,8,128]{2,1,0:T(8,128)} %coarse.1), calls=%async_computation | async-start | bytes 262144 | tf_op jit(solution)/shard_map/all_to_all | solution.py:267
  9.5 0.0 copy-done
  9.5 0.0 copy-done.1
  9.5 0.0 copy-start.2
  9.5 0.7 %copy-done.2 = f32[64,64]{1,0:T(8,128)S(1)} copy-done((f32[64,64]{1,0:T(8,128)S(1)}, f32[64,64]{1,0:T(8,128)}, u32[]{:S(2)}) %copy-start.2) | copy-done | bytes 16408
  10.3 2.0 %matrices.1 = (bf16[4,384,192]{2,1,0:T(8,128)(2,1)S(1)}, bf16[33,128,96]{2,1,0:T(8,128)(2,1)S(1)}) custom-call(f32[64,64]{1,0:T(8,128)S(1)} %copy-done.2, f32[8,64,64]{2,1,0:T(8,128)S(1)} %copy-done, f32[16,64,64]{2,1,0:T(8,128)S(1)} %copy-done.1), custom_call_target="tpu_custom_call" | custom-call | tf_op jit(solution)/shard_map/matrices/pallas_call | solution.py:268
  12.2 5.5 %all-to-all-done.refs_0_ = f32[32,8,128]{2,1,0:T(8,128)S(1)} async-done(((f32[32,8,128]{2,1,0:T(8,128)}), f32[32,8,128]{2,1,0:T(8,128)S(1)}, u32[]{:S(2)}, u32[]{:S(2)}) %all-to-all-start) | async-done | bytes 131104 | tf_op jit(solution)/shard_map/all_to_all | solution.py:267
  17.7 6.0 %solve.1 = f32[32,16,128]{2,1,0:T(8,128)S(1)} custom-call(f32[32,8,128]{2,1,0:T(8,128)S(1)} %all-to-all-done.refs_0_, bf16[4,384,192]{2,1,0:T(8,128)(2,1)S(1)} %get-tuple-element.7.refs_1_, bf16[33,128,96]{2,1,0:T(8,128)(2,1)S(1)} %get-tuple-element.8.refs_2_), custom_call_target="tpu_custom_call" | custom-call | tf_op jit(solution)/shard_map/solve/pallas_call | solution.py:280
  23.7 12.2 %all_to_all.10.got = f32[32,16,128]{2,1,0:T(8,128)S(1)} all-to-all(f32[32,16,128]{2,1,0:T(8,128)S(1)} %solve.1), channel_id=1, replica_groups=mesh['slab'=4,'grp'=8] {'slab','grp'}, dimensions={0} | all-to-all | bytes 524288 | tf_op jit(solution)/shard_map/all_to_all | solution.py:296
  35.8 0.9 %finish.1 = f32[8,64,128]{2,1,0:T(8,128)} custom-call(f32[32,16,128]{2,1,0:T(8,128)S(1)} %all_to_all.10.got), custom_call_target="tpu_custom_call" | custom-call | tf_op jit(solution)/shard_map/finish/pallas_call | solution.py:297
Async XLA Ops:
  0.0 9.5 %copy-start = (f32[8,64,64]{2,1,0:T(8,128)S(1)}, f32[8,64,64]{2,1,0:T(8,128)}, u32[]{:S(2)}) copy-start(f32[8,64,64]{2,1,0:T(8,128)} %prolong.3) | copy-start | bytes 393220
  0.0 9.5 %copy-start.1 = (f32[16,64,64]{2,1,0:T(8,128)S(1)}, f32[16,64,64]{2,1,0:T(8,128)}, u32[]{:S(2)}) copy-start(f32[16,64,64]{2,1,0:T(8,128)} %penalty.1) | copy-start | bytes 786436
  2.4 15.3 %all-to-all-start = ((f32[32,8,128]{2,1,0:T(8,128)}), f32[32,8,128]{2,1,0:T(8,128)S(1)}, u32[]{:S(2)}, u32[]{:S(2)}) async-start(f32[32,8,128]{2,1,0:T(8,128)} %coarse.1), calls=%async_computation | async-start | bytes 262144 | tf_op jit(solution)/shard_map/all_to_all | solution.py:267
  9.5 0.8 %copy-start.2 = (f32[64,64]{1,0:T(8,128)S(1)}, f32[64,64]{1,0:T(8,128)}, u32[]{:S(2)}) copy-start(f32[64,64]{1,0:T(8,128)} %stiffness.1) | copy-start | bytes 49156

commit v3 on v2

--- a/solution.py
+++ b/solution.py
@@ -91,16 +91,21 @@
         extra[m : m + 1, 0:dof] = jnp.sum(mat * eye, axis=0, keepdims=True)
         mall[m, :, 0:dof] = mat[:half]
         mall[m, :, dof : 2 * dof] = mat[half:]
-        hi, lo = halves(mat)
-        wide = jnp.concatenate([hi, hi, lo], axis=1)
-        for g in range(GROUPS):
-            stacked[g, m * rows : (m + 1) * rows, :] = wide[g * rows : (g + 1) * rows]
     for pair in range(half + 1):
-        hi, lo = halves(mall[:, pair, :] if pair < half else extra[...])
+        both = mall[:, pair, :] if pair < half else extra[...]
+        hi, lo = halves(both)
         columns[pair] = jnp.concatenate([hi, hi, lo], axis=0).T
-
-
-def solve_kernel(strides, got, stacked, columns, out, flat, resid, update, answer, coefs, tiles):
+        if pair < half:
+            for place in range(2):
+                row = pair + place * half
+                cut = slice(place * dof, (place + 1) * dof)
+                g, first = row // rows, row % rows * (kids + codes)
+                stacked[g, first : first + kids + codes, :] = jnp.concatenate(
+                    [hi[: kids + codes, cut], hi[: kids + codes, cut], lo[: kids + codes, cut]], axis=1
+                )
+
+
+def solve_kernel(strides, got, stacked, columns, out, flat, resid, update, answer, tiles):
     count = got.shape[1] // 2
     members = got.shape[0]
     total = members * count
@@ -114,23 +119,44 @@
     facts = flat[1].T
     dens = facts[0:kids]
     slots = facts[kids : 2 * kids]
-    open_face = facts[2 * kids : 2 * kids + FACES] > 0.5
-    codes = facts[3 * kids : 3 * kids + FACES].astype(jnp.int32)
+    open_face = facts[2 * kids : 3 * kids] > 0.5
+    codes = facts[3 * kids : 4 * kids].astype(jnp.int32)
     rho = jnp.sum(dens, axis=0, keepdims=True) * f32(1.0 / kids)
     inverse = 1.0 / dens
-    place = lax.broadcasted_iota(jnp.int32, (kids, total), 0).astype(f32)
+    place = lax.broadcasted_iota(jnp.int32, (kids, total), 0)
     weight = jnp.zeros((kids, total), f32)
     for q in range(kids):
-        weight = weight + jnp.where(slots[q : q + 1] == place, inverse[q : q + 1], 0.0)
+        weight = weight + jnp.where(slots[q : q + 1] == place.astype(f32), inverse[q : q + 1], 0.0)
     shifts = [sign * stride for stride in strides for sign in (-1, 1)]
+    lane = lax.broadcasted_iota(jnp.int32, (kids, total), 1)
+
+    def across(x, flip):
+        if total == LANES:
+            moved = lane
+            for f in range(FACES):
+                moved = jnp.where(place == f, lane + shifts[f ^ flip], moved)
+            return jnp.take_along_axis(x, moved & (total - 1), axis=1)
+        moved = jnp.zeros(x.shape, x.dtype)
+        for f in range(FACES):
+            moved = jnp.where(place == f, pltpu.roll(x, (-shifts[f ^ flip]) % total, 1), moved)
+        return moved
+
+    def pick(x, rows_of):
+        return jnp.concatenate(
+            [
+                jnp.take_along_axis(
+                    x[:, t * LANES : (t + 1) * LANES], rows_of[:, t * LANES : (t + 1) * LANES], axis=0
+                )
+                for t in range(total // LANES)
+            ],
+            axis=1,
+        )
+
+    face_w = jnp.where(open_face, 2.0 / (rho + across(jnp.broadcast_to(rho, (kids, total)), 0)), 0.0)
     code_place = lax.broadcasted_iota(jnp.int32, (16, total), 0)
     face_sum = jnp.zeros((16, total), f32)
-    face_w = []
     for f in range(FACES):
-        other = pltpu.roll(rho, (-shifts[f]) % total, 1)
-        fw = jnp.where(open_face[f : f + 1], 2.0 / (rho + other), 0.0)
-        face_w.append(fw)
-        face_sum = face_sum + jnp.where(codes[f : f + 1] == code_place, fw, 0.0)
+        face_sum = face_sum + jnp.where(codes[f : f + 1] == code_place, face_w[f : f + 1], 0.0)
     coef = jnp.concatenate([weight, face_sum, jnp.zeros((8, total), f32)], axis=0)
     c_hi, c_lo = halves(coef)
     c_all = jnp.concatenate([c_hi, c_lo, c_hi], axis=0)
@@ -147,18 +173,13 @@
     sigma = centre / half_width
     damping = 1.0 / sigma
     inv_jac = 1.0 / jacobi
-    inv_jac = jnp.concatenate([inv_jac, inv_jac], axis=1)
     start = jnp.concatenate([coarse[:dof], coarse[dof:]], axis=1)
     resid[...] = start
-    start = start * inv_jac / centre
+    start = start * jnp.concatenate([inv_jac, inv_jac], axis=1) / centre
     update[...] = start
     answer[...] = start
-    for f in range(FACES):
-        coefs[f : f + 1, :] = jnp.concatenate([face_w[f], face_w[f]], axis=1)
-        fc = codes[f : f + 1].astype(f32)
-        coefs[8 + f : 9 + f, :] = jnp.concatenate([fc, fc], axis=1)
-    coefs[16:24, :] = jnp.concatenate([weight, weight], axis=1)
-    jac2 = inv_jac
+    code_row = codes & 7
+    upper_half = codes > 7
 
     def sweep(_, damp):
         hi, lo = halves(update[...])
@@ -168,37 +189,33 @@
         gain = 2.0 * damp_next / half_width
         for g in range(GROUPS):
             prod = jnp.dot(stacked[g], right, preferred_element_type=f32)
-            mats = [prod[m * rows : (m + 1) * rows] for m in range(24)]
-            applied = coefs[16:17] * mats[0]
-            for s in range(1, kids):
-                applied = applied + coefs[16 + s : 17 + s] * mats[s]
-            terms = []
-            for f in range(FACES):
-                fc = coefs[8 + f : 9 + f].astype(jnp.int32)
-                fc = jnp.broadcast_to(fc, (rows, 2 * total))
-                level = mats[kids:]
-                for bit in range(4):
-                    on = ((fc >> bit) & 1) > 0
-                    level = [
-                        jnp.where(on, level[2 * n + 1], level[2 * n]) for n in range(len(level) // 2)
-                    ]
-                terms.append(coefs[f : f + 1] * level[0])
-            for f in range(FACES):
-                moved = terms[f ^ 1]
-                moved = jnp.concatenate(
-                    [
-                        pltpu.roll(moved[:, :total], (-shifts[f]) % total, 1),
-                        pltpu.roll(moved[:, total:], (-shifts[f]) % total, 1),
-                    ],
-                    axis=1,
-                )
-                applied = applied + (terms[f] - moved)
-            part = pl.ds(g * rows, rows)
-            left = resid[part, :] - applied
-            resid[part, :] = left
-            new = keep * update[part, :] + gain * (left * jac2[g * rows : (g + 1) * rows])
-            update[part, :] = new
-            answer[part, :] = answer[part, :] + new
+            for first in range(0, rows, 8):
+                for c in range(2):
+                    cut = slice(c * total, (c + 1) * total)
+                    sums = []
+                    for n in range(8):
+                        base = (first + n) * 24
+                        face = jnp.where(
+                            upper_half,
+                            pick(prod[base + 16 : base + 24, cut], code_row),
+                            pick(prod[base + 8 : base + 16, cut], code_row),
+                        )
+                        face = face * face_w
+                        sums.append(prod[base : base + 8, cut] * weight + (face - across(face, 1)))
+                    for bit in (4, 2, 1):
+                        clear = (place & bit) == 0
+                        sums = [
+                            jnp.where(clear, sums[n], sums[n + bit])
+                            + pick(jnp.where(clear, sums[n + bit], sums[n]), place ^ bit)
+                            for n in range(bit)
+                        ]
+                    part = pl.ds(g * rows + first, 8)
+                    left = resid[part, cut] - sums[0]
+                    resid[part, cut] = left
+                    inv = inv_jac[g * rows + first : g * rows + first + 8]
+                    new = keep * update[part, cut] + gain * (left * inv)
+                    update[part, cut] = new
+                    answer[part, cut] = answer[part, cut] + new
         return damp_next
 
     lax.fori_loop(0, SWEEPS, sweep, damping)
@@ -287,7 +304,6 @@
             pltpu.VMEM((dof, 2 * total), f32),
             pltpu.VMEM((dof, 2 * total), f32),
             pltpu.VMEM((dof, 2 * total), f32),
-            pltpu.VMEM((24, 2 * total), f32),
             pltpu.VMEM((2 * total // LANES, dof, LANES), f32),
         ],
         compiler_params=pltpu.CompilerParams(vmem_limit_bytes=40 << 20),

time: 37 us -> 35.8 us (0.968)
  Pallas kernels: 11.2 us -> 9.93 us
    pallas_call x1, Pallas kernels: 5.98 us -> 4.74 us  [local(): pl.pallas_call(lambda *refs: solve_kernel(strides, *refs), out_shape=pltp...]
where the time goes in v3:
time: 35.8 us; the launch traced here: 35.5 us
  blocking collectives  12.2 us (34%)
  Pallas kernels  9.93 us (28%)
  starting transfers between devices  7.08 us (20%)
  waiting for transfers between devices  5.53 us (15%)
  local copies, waits for them, and re-layouts  0.76 us (2%)
    all_to_all x1, blocking collectives, local(): back = lax.all_to_all(back, every, 0, 0, tiled=True)  12.2 us
    all_to_all x1, starting transfers between devices, local(): got = lax.all_to_all(sent, every, 0, 0, tiled=True)  7.08 us
    all_to_all x1, waiting for transfers between devices, local(): got = lax.all_to_all(sent, every, 0, 0, tiled=True)  5.53 us
    pallas_call x1, Pallas kernels, local(): pl.pallas_call(lambda *refs: solve_kernel(strides, *refs), out_shape=pltp...  4.74 us
    pallas_call x1, Pallas kernels, local(): pl.pallas_call(coarse_kernel, out_shape=pltpu.VMEM((members, 2 * count, L...  2.38 us
    pallas_call x1, Pallas kernels, local(): pl.pallas_call(matrices_kernel, out_shape=(pltpu.VMEM((GROUPS, 24 * (dof...  1.9 us
    pallas_call x1, Pallas kernels, local(): pl.pallas_call(finish_kernel, out_shape=jax.ShapeDtypeStruct((slabs * row...  0.91 us
    unnamed x6, local copies, waits for them, and re-layouts  0.76 us
  transfers between devices with their start and end apart: 1, of which 1 were waited for; matrix products, arithmetic and copies ran while one was open for 0% of the time, Pallas kernels for 5%

profile of v3, /device:TPU:1, one launch (start us, length us, event | category | flops | bytes accessed | tf_op | source)
XLA Modules:
  0.0 35.5 jit_solution(10767116862141373672)
XLA Ops:
  0.0 0.0 copy-start
  0.0 0.0 copy-start.1
  0.0 2.4 %coarse.1 = f32[32,8,128]{2,1,0:T(8,128)} custom-call(s32[1,2,2,8]{3,2,1,0:T(2,128)} %slot_v.1, f32[1,2,2,8]{3,2,1,0:T(2,128)} %dens.1, s32[1,2,2,8]{3,2,1,0:T(2,128)} %slot_v.1, s32[1,2,2,6]{3,2,1,0:T(2,128)} %links.1, s32[1,2,2,6]{3,2,1,0:T(2,128)} %code.1, f32[8,64,64]{2,1,0:T(8,128)} %prolong.3, bf16[1,2,2,8,4096]{4,3,2,1,0:T(8,128)(2,1)} %rhs.1), custom_call_target="tpu_custom_call" | custom-call | tf_op jit(solution)/shard_map/coarse/pallas_call | solution.py:271
  2.4 7.1 %all-to-all-start = ((f32[32,8,128]{2,1,0:T(8,128)}), f32[32,8,128]{2,1,0:T(8,128)S(1)}, u32[]{:S(2)}, u32[]{:S(2)}) async-start(f32[32,8,128]{2,1,0:T(8,128)} %coarse.1), calls=%async_computation | async-start | bytes 262144 | tf_op jit(solution)/shard_map/all_to_all | solution.py:284
  9.5 0.0 copy-done
  9.5 0.0 copy-done.1
  9.5 0.0 copy-start.2
  9.5 0.7 %copy-done.2 = f32[64,64]{1,0:T(8,128)S(1)} copy-done((f32[64,64]{1,0:T(8,128)S(1)}, f32[64,64]{1,0:T(8,128)}, u32[]{:S(2)}) %copy-start.2) | copy-done | bytes 16408
  10.3 1.9 %matrices.1 = (bf16[4,384,192]{2,1,0:T(8,128)(2,1)S(1)}, bf16[33,128,96]{2,1,0:T(8,128)(2,1)S(1)}) custom-call(f32[64,64]{1,0:T(8,128)S(1)} %copy-done.2, f32[8,64,64]{2,1,0:T(8,128)S(1)} %copy-done, f32[16,64,64]{2,1,0:T(8,128)S(1)} %copy-done.1), custom_call_target="tpu_custom_call" | custom-call | tf_op jit(solution)/shard_map/matrices/pallas_call | solution.py:285
  12.2 5.5 %all-to-all-done.refs_0_ = f32[32,8,128]{2,1,0:T(8,128)S(1)} async-done(((f32[32,8,128]{2,1,0:T(8,128)}), f32[32,8,128]{2,1,0:T(8,128)S(1)}, u32[]{:S(2)}, u32[]{:S(2)}) %all-to-all-start) | async-done | bytes 131104 | tf_op jit(solution)/shard_map/all_to_all | solution.py:284
  17.7 4.7 %solve.1 = f32[32,16,128]{2,1,0:T(8,128)S(1)} custom-call(f32[32,8,128]{2,1,0:T(8,128)S(1)} %all-to-all-done.refs_0_, bf16[4,384,192]{2,1,0:T(8,128)(2,1)S(1)} %get-tuple-element.7.refs_1_, bf16[33,128,96]{2,1,0:T(8,128)(2,1)S(1)} %get-tuple-element.8.refs_2_), custom_call_target="tpu_custom_call" | custom-call | tf_op jit(solution)/shard_map/solve/pallas_call | solution.py:297
  22.4 12.2 %all_to_all.10.got = f32[32,16,128]{2,1,0:T(8,128)S(1)} all-to-all(f32[32,16,128]{2,1,0:T(8,128)S(1)} %solve.1), channel_id=1, replica_groups=mesh['slab'=4,'grp'=8] {'slab','grp'}, dimensions={0} | all-to-all | bytes 524288 | tf_op jit(solution)/shard_map/all_to_all | solution.py:312
  34.6 0.9 %finish.1 = f32[8,64,128]{2,1,0:T(8,128)} custom-call(f32[32,16,128]{2,1,0:T(8,128)S(1)} %all_to_all.10.got), custom_call_target="tpu_custom_call" | custom-call | tf_op jit(solution)/shard_map/finish/pallas_call | solution.py:313
Async XLA Ops:
  0.0 9.5 %copy-start = (f32[8,64,64]{2,1,0:T(8,128)S(1)}, f32[8,64,64]{2,1,0:T(8,128)}, u32[]{:S(2)}) copy-start(f32[8,64,64]{2,1,0:T(8,128)} %prolong.3) | copy-start | bytes 393220
  0.0 9.5 %copy-start.1 = (f32[16,64,64]{2,1,0:T(8,128)S(1)}, f32[16,64,64]{2,1,0:T(8,128)}, u32[]{:S(2)}) copy-start(f32[16,64,64]{2,1,0:T(8,128)} %penalty.1) | copy-start | bytes 786436
  2.4 15.3 %all-to-all-start = ((f32[32,8,128]{2,1,0:T(8,128)}), f32[32,8,128]{2,1,0:T(8,128)S(1)}, u32[]{:S(2)}, u32[]{:S(2)}) async-start(f32[32,8,128]{2,1,0:T(8,128)} %coarse.1), calls=%async_computation | async-start | bytes 262144 | tf_op jit(solution)/shard_map/all_to_all | solution.py:284
  9.5 0.8 %copy-start.2 = (f32[64,64]{1,0:T(8,128)S(1)}, f32[64,64]{1,0:T(8,128)}, u32[]{:S(2)}) copy-start(f32[64,64]{1,0:T(8,128)} %stiffness.1) | copy-start | bytes 49156

commit v4 on v3

--- a/solution.py
+++ b/solution.py
@@ -25,33 +25,64 @@
     return lax.dot_general(a, b, (((0,), (0,)), ((), ())), preferred_element_type=f32)
 
 
-def coarse_kernel(slot_s, dens, slot_v, links, code, prolong, rhs, out, wide, pairs, weights, info):
+def coarse_kernel(
+    dens_h, slot_h, links_h, code_h, stiffness_h, prolong_h, penalty_h, rhs_h,
+    out, stiff, prolong, penalty,
+    slot_s, dens, slot_v, links, code, rhs, wide, pairs, weights, info, sems,
+):
+    moves = [
+        pltpu.make_async_copy(source, target, sems.at[n])
+        for n, (source, target) in enumerate(
+            [
+                (prolong_h, prolong),
+                (slot_h, slot_s),
+                (rhs_h, rhs),
+                (dens_h, dens),
+                (slot_h, slot_v),
+                (links_h, links),
+                (code_h, code),
+                (penalty_h, penalty),
+                (stiffness_h, stiff),
+            ]
+        )
+    ]
+    for move in moves:
+        move.start()
     kids, dof, _ = prolong.shape
     half = dof // 2
     _, rows_b, rows_c, _ = dens.shape
     count = rows_b * rows_c
-    members = out.shape[0]
+    span = count + 1
+    members = out.shape[0] // span
     groups = half
+    wide_fact = LANES // count
     info[...] = jnp.zeros(info.shape, f32)
-    for a in range(count):
-        b, c = a // rows_c, a % rows_c
-        info[a : a + 1, 0:kids] = dens[0, b, c : c + 1, :]
-        info[a : a + 1, kids : 2 * kids] = slot_v[0, b, c : c + 1, :].astype(f32)
-        info[a : a + 1, 2 * kids : 2 * kids + FACES] = jnp.where(
-            links[0, b, c : c + 1, :] >= 0, f32(1.0), f32(0.0)
-        )
-        info[a : a + 1, 3 * kids : 3 * kids + FACES] = code[0, b, c : c + 1, :].astype(f32)
-    out[:, count : 2 * count, :] = jnp.broadcast_to(info[0:count, :][None], (members, count, LANES))
+    moves[0].wait()
     first_half = lax.broadcasted_iota(jnp.int32, (half, LANES), 1) < dof
     for s in range(kids):
         wide[s, :, 0:dof] = prolong[s]
         even = wide[s, pl.ds(0, half, stride=2), :]
         odd = wide[s, pl.ds(1, half, stride=2), :]
         pairs[s] = jnp.where(first_half, even, pltpu.roll(odd, dof, 1))
+    moves[1].wait()
     for a in range(count):
         b, c = a // rows_c, a % rows_c
         for q in range(kids):
             weights[a, pl.ds(q, half, stride=kids), :] = pairs[slot_s[0, b, c, q]]
+    for move in moves[2:7]:
+        move.wait()
+    for a in range(count):
+        b, c = a // rows_c, a % rows_c
+        base = a * wide_fact
+        info[0:1, base : base + kids] = dens[0, b, c : c + 1, :]
+        info[0:1, base + kids : base + 2 * kids] = slot_v[0, b, c : c + 1, :].astype(f32)
+        info[0:1, base + 2 * kids : base + 2 * kids + FACES] = jnp.where(
+            links[0, b, c : c + 1, :] >= 0, f32(1.0), f32(0.0)
+        )
+        info[0:1, base + 3 * kids : base + 3 * kids + FACES] = code[0, b, c : c + 1, :].astype(f32)
+    facts = jnp.broadcast_to(info[0:1, :], (groups, LANES))
+    for first in range(0, members, groups):
+        out[pl.ds(first * span + count, groups, stride=span), :] = facts
     for a in range(count):
         b, c = a // rows_c, a % rows_c
         cells = rhs[0, b, c].astype(f32)
@@ -62,7 +93,9 @@
         own = prod[:dof, :dof] + prod[dof:, dof:]
         row = jnp.concatenate([own[:groups], own[groups:]], axis=1)
         for first in range(0, members, groups):
-            out[first : first + groups, a, :] = row
+            out[pl.ds(first * span + a, groups, stride=span), :] = row
+    for move in moves[7:]:
+        move.wait()
 
 
 def matrices_kernel(stiffness, prolong, penalty, stacked, columns, mall, extra):
@@ -91,10 +124,15 @@
         extra[m : m + 1, 0:dof] = jnp.sum(mat * eye, axis=0, keepdims=True)
         mall[m, :, 0:dof] = mat[:half]
         mall[m, :, dof : 2 * dof] = mat[half:]
+    parts = []
     for pair in range(half + 1):
         both = mall[:, pair, :] if pair < half else extra[...]
         hi, lo = halves(both)
-        columns[pair] = jnp.concatenate([hi, hi, lo], axis=0).T
+        parts.append(jnp.concatenate([hi, hi, lo], axis=0))
+        if pair % 2:
+            columns[pair // 2] = jnp.concatenate(parts[pair - 1 :], axis=0).T
+        elif pair == half:
+            columns[pair // 2] = jnp.concatenate([parts[pair], jnp.zeros_like(parts[pair])], axis=0).T
         if pair < half:
             for place in range(2):
                 row = pair + place * half
@@ -106,15 +144,19 @@
 
 
 def solve_kernel(strides, got, stacked, columns, out, flat, resid, update, answer, tiles):
-    count = got.shape[1] // 2
-    members = got.shape[0]
-    total = members * count
+    total = flat.shape[1]
+    span = got.shape[0] // out.shape[0]
+    count = span - 1
+    members = out.shape[0]
+    wide_fact = LANES // count
     dof = resid.shape[0]
     kids = 8
     rows = dof // GROUPS
+    everyone = got[pl.ds(count, members, stride=span), :]
     for a in range(count):
-        flat[0, pl.ds(a, members, stride=count), :] = got[:, a, :]
-        flat[1, pl.ds(a, members, stride=count), :] = got[:, count + a, :]
+        flat[0, pl.ds(a, members, stride=count), :] = got[pl.ds(a, members, stride=span), :]
+        own = pltpu.roll(everyone, LANES - a * wide_fact, 1) if a else everyone
+        flat[1, pl.ds(a, members, stride=count), :] = own
     coarse = flat[0].T
     facts = flat[1].T
     dens = facts[0:kids]
@@ -160,12 +202,17 @@
     coef = jnp.concatenate([weight, face_sum, jnp.zeros((8, total), f32)], axis=0)
     c_hi, c_lo = halves(coef)
     c_all = jnp.concatenate([c_hi, c_lo, c_hi], axis=0)
-    last = jnp.dot(columns[dof // 2], c_all, preferred_element_type=f32)
-    jacobi = last[:dof]
-    sums = last[dof:]
-    for pair in range(dof // 2):
-        part = jnp.abs(jnp.dot(columns[pair], c_all, preferred_element_type=f32))
-        sums = sums + (part[:dof] + part[dof:])
+    nothing = jnp.zeros_like(c_all)
+    c_two = jnp.concatenate(
+        [jnp.concatenate([c_all, nothing], axis=1), jnp.concatenate([nothing, c_all], axis=1)], axis=0
+    )
+    last = jnp.dot(columns[dof // 4], c_two, preferred_element_type=f32)
+    jacobi = last[:dof, :total]
+    sums = last[dof:, :total]
+    for pair in range(dof // 4):
+        part = jnp.abs(jnp.dot(columns[pair], c_two, preferred_element_type=f32))
+        part = part[:dof] + part[dof:]
+        sums = sums + (part[:, :total] + part[:, total:])
     upper = jnp.max(jnp.max(sums / jacobi, axis=0, keepdims=True), axis=1, keepdims=True)
     lower = upper / 10.0
     centre = 0.5 * (upper + lower)
@@ -268,32 +315,53 @@
     total = members * count
     every = ("slab", "grp")
     strides = (grps * count, rows_c, 1)
-    sent = pl.pallas_call(
+    anywhere = pl.BlockSpec(memory_space=pl.ANY)
+    codes = penalty.shape[0]
+    sent, stiff, prol, pen = pl.pallas_call(
         coarse_kernel,
-        out_shape=pltpu.VMEM((members, 2 * count, LANES), f32),
-        in_specs=[pl.BlockSpec(memory_space=pltpu.SMEM)] + [vmem()] * 6,
-        out_specs=vmem(),
+        out_shape=(
+            pltpu.HBM((members * (count + 1), LANES), f32),
+            pltpu.VMEM((dof, dof), f32),
+            pltpu.VMEM((kids, dof, dof), f32),
+            pltpu.VMEM((codes, dof, dof), f32),
+        ),
+        in_specs=[anywhere] * 8,
+        out_specs=(vmem(), vmem(), vmem(), vmem()),
         scratch_shapes=[
+            pltpu.SMEM(cell_slot.shape, jnp.int32),
+            pltpu.VMEM(cell_density.shape, f32),
+            pltpu.VMEM(cell_slot.shape, jnp.int32),
+            pltpu.VMEM(neighbours.shape, jnp.int32),
+            pltpu.VMEM(face_code.shape, jnp.int32),
+            pltpu.VMEM(fine_rhs.shape, bf16),
             pltpu.VMEM((kids, dof, LANES), f32),
             pltpu.VMEM((kids, dof // 2, LANES), f32),
             pltpu.VMEM((count, kids * dof // 2, LANES), f32),
             pltpu.VMEM((8, LANES), f32),
+            pltpu.SemaphoreType.DMA((9,)),
         ],
+        compiler_params=pltpu.CompilerParams(vmem_limit_bytes=24 << 20),
         name="coarse",
-    )(cell_slot, cell_density, cell_slot, neighbours, face_code, prolong, fine_rhs)
-    got = lax.all_to_all(sent, every, 0, 0, tiled=True)
+    )(
+        *[
+            pltpu.with_memory_space_constraint(x, pltpu.HBM)
+            for x in (cell_density, cell_slot, neighbours, face_code, stiffness, prolong, penalty, fine_rhs)
+        ]
+    )
+    got = lax.all_to_all(sent.reshape(members, 1, (count + 1) * LANES), every, 0, 0, tiled=True)
+    got = got.reshape(members * (count + 1), LANES)
     stacked, columns = pl.pallas_call(
         matrices_kernel,
         out_shape=(
             pltpu.VMEM((GROUPS, 24 * (dof // GROUPS), 3 * dof), bf16),
-            pltpu.VMEM((dof // 2 + 1, 2 * dof, 3 * PADM), bf16),
+            pltpu.VMEM((dof // 4 + 1, 2 * dof, 6 * PADM), bf16),
         ),
         in_specs=[vmem()] * 3,
         out_specs=(vmem(), vmem()),
         scratch_shapes=[pltpu.VMEM((PADM, dof // 2, 2 * dof), f32), pltpu.VMEM((PADM, 2 * dof), f32)],
         compiler_params=pltpu.CompilerParams(vmem_limit_bytes=24 << 20),
         name="matrices",
-    )(near(stiffness), near(prolong), near(penalty))
+    )(near(stiff), near(prol), near(pen))
     back = pl.pallas_call(
         lambda *refs: solve_kernel(strides, *refs),
         out_shape=pltpu.VMEM((members, 4 * slabs, LANES), f32),

time: 35.8 us -> 35.1 us (0.980)
  local copies, waits for them, and re-layouts: 0.76 us -> 0 us
    unnamed x6 -> x0, local copies, waits for them, and re-layouts: 0.76 us -> none
  transfers between devices with their start and end apart: 1 -> 1, of which waited for: 1 -> 1; matrix products, arithmetic and copies ran while one was open for 0% -> 0% of each run, Pallas kernels for 5% -> 6%
where the time goes in v4:
time: 35.1 us; the launch traced here: 34.9 us
  blocking collectives  12.3 us (35%)
  Pallas kernels  9.96 us (28%)
  starting transfers between devices  7.09 us (20%)
  waiting for transfers between devices  5.48 us (16%)
    all_to_all x1, blocking collectives, local(): back = lax.all_to_all(back, every, 0, 0, tiled=True)  12.3 us
    all_to_all x1, starting transfers between devices, local(): lax.all_to_all(sent.reshape(members, 1, (count + 1) * LANES), every, 0, 0...  7.09 us
    all_to_all x1, waiting for transfers between devices, local(): lax.all_to_all(sent.reshape(members, 1, (count + 1) * LANES), every, 0, 0...  5.48 us
    pallas_call x1, Pallas kernels, local(): pl.pallas_call(lambda *refs: solve_kernel(strides, *refs), out_shape=pltp...  4.81 us
    pallas_call x1, Pallas kernels, local(): pl.pallas_call(coarse_kernel, out_shape=(pltpu.HBM((members * (count + 1)...  2.3 us
    pallas_call x1, Pallas kernels, local(): pl.pallas_call(matrices_kernel, out_shape=(pltpu.VMEM((GROUPS, 24 * (dof...  1.93 us
    pallas_call x1, Pallas kernels, local(): pl.pallas_call(finish_kernel, out_shape=jax.ShapeDtypeStruct((slabs * row...  0.91 us
  transfers between devices with their start and end apart: 1, of which 1 were waited for; matrix products, arithmetic and copies ran while one was open for 0% of the time, Pallas kernels for 6%

profile of v4, /device:TPU:1, one launch (start us, length us, event | category | flops | bytes accessed | tf_op | source)
XLA Modules:
  0.0 34.9 jit_solution(9617024982390374571)
XLA Ops:
  0.0 2.3 %coarse.1 = (f32[160,128]{1,0:T(8,128)}, f32[64,64]{1,0:T(8,128)S(1)}, f32[8,64,64]{2,1,0:T(8,128)S(1)}, f32[16,64,64]{2,1,0:T(8,128)S(1)}) custom-call(f32[1,2,2,8]{3,2,1,0:T(2,128)} %dens_h.1, s32[1,2,2,8]{3,2,1,0:T(2,128)} %slot_h.1, s32[1,2,2,6]{3,2,1,0:T(2,128)} %links_h.1, s32[1,2,2,6]{3,2,1,0:T(2,128)} %code_h.1, f32[64,64]{1,0:T(8,128)} %stiffness_h.1, ...), custom_call_target="tpu_custom_call" | custom-call | tf_op jit(solution)/shard_map/coarse/pallas_call | solution.py:320
  2.3 7.1 %all-to-all-start = ((f32[32,1,640]{2,1,0:T(1,128)}), f32[32,1,640]{2,1,0:T(1,128)S(1)}, u32[]{:S(2)}, u32[]{:S(2)}) async-start(f32[32,1,640]{2,1,0:T(1,128)} %bitcast.8), calls=%async_computation | async-start | bytes 163840 | tf_op jit(solution)/shard_map/all_to_all | solution.py:351
  9.4 1.9 %matrices.1 = (bf16[4,384,192]{2,1,0:T(8,128)(2,1)S(1)}, bf16[17,128,192]{2,1,0:T(8,128)(2,1)S(1)}) custom-call(f32[64,64]{1,0:T(8,128)S(1)} %get-tuple-element.12.stiffness, f32[8,64,64]{2,1,0:T(8,128)S(1)} %get-tuple-element.13.prolong, f32[16,64,64]{2,1,0:T(8,128)S(1)} %get-tuple-element.14.penalty), custom_call_target="tpu_custom_call" | custom-call | tf_op jit(solution)/shard_map/matrices/pallas_call | solution.py:353
  11.3 5.5 %all-to-all-done = f32[32,1,640]{2,1,0:T(1,128)S(1)} async-done(((f32[32,1,640]{2,1,0:T(1,128)}), f32[32,1,640]{2,1,0:T(1,128)S(1)}, u32[]{:S(2)}, u32[]{:S(2)}) %all-to-all-start) | async-done | bytes 81952 | tf_op jit(solution)/shard_map/all_to_all | solution.py:351
  16.8 4.8 %solve.1 = f32[32,16,128]{2,1,0:T(8,128)S(1)} custom-call(f32[160,128]{1,0:T(8,128)S(1)} %bitcast.7, bf16[4,384,192]{2,1,0:T(8,128)(2,1)S(1)} %get-tuple-element.15.refs_1_, bf16[17,128,192]{2,1,0:T(8,128)(2,1)S(1)} %get-tuple-element.16.refs_2_), custom_call_target="tpu_custom_call" | custom-call | tf_op jit(solution)/shard_map/solve/pallas_call | solution.py:365
  21.7 12.3 %all_to_all.10.got = f32[32,16,128]{2,1,0:T(8,128)S(1)} all-to-all(f32[32,16,128]{2,1,0:T(8,128)S(1)} %solve.1), channel_id=1, replica_groups=mesh['slab'=4,'grp'=8] {'slab','grp'}, dimensions={0} | all-to-all | bytes 524288 | tf_op jit(solution)/shard_map/all_to_all | solution.py:380
  34.0 0.9 %finish.1 = f32[8,64,128]{2,1,0:T(8,128)} custom-call(f32[32,16,128]{2,1,0:T(8,128)S(1)} %all_to_all.10.got), custom_call_target="tpu_custom_call" | custom-call | tf_op jit(solution)/shard_map/finish/pallas_call | solution.py:381
Async XLA Ops:
  2.3 14.5 %all-to-all-start = ((f32[32,1,640]{2,1,0:T(1,128)}), f32[32,1,640]{2,1,0:T(1,128)S(1)}, u32[]{:S(2)}, u32[]{:S(2)}) async-start(f32[32,1,640]{2,1,0:T(1,128)} %bitcast.8), calls=%async_computation | async-start | bytes 163840 | tf_op jit(solution)/shard_map/all_to_all | solution.py:351

commit v5 on v4

--- a/solution.py
+++ b/solution.py
@@ -214,26 +214,19 @@
         part = part[:dof] + part[dof:]
         sums = sums + (part[:, :total] + part[:, total:])
     upper = jnp.max(jnp.max(sums / jacobi, axis=0, keepdims=True), axis=1, keepdims=True)
-    lower = upper / 10.0
-    centre = 0.5 * (upper + lower)
-    half_width = 0.5 * (upper - lower)
-    sigma = centre / half_width
-    damping = 1.0 / sigma
-    inv_jac = 1.0 / jacobi
+    inv_jac = 1.0 / (jacobi * upper)
+    sigma = 11.0 / 9.0
     start = jnp.concatenate([coarse[:dof], coarse[dof:]], axis=1)
     resid[...] = start
-    start = start * jnp.concatenate([inv_jac, inv_jac], axis=1) / centre
+    start = start * jnp.concatenate([inv_jac, inv_jac], axis=1) * f32(1.0 / 0.55)
     update[...] = start
     answer[...] = start
     code_row = codes & 7
     upper_half = codes > 7
 
-    def sweep(_, damp):
+    def sweep(keep, gain):
         hi, lo = halves(update[...])
         right = jnp.concatenate([hi, lo, hi], axis=0)
-        damp_next = 1.0 / (2.0 * sigma - damp)
-        keep = damp_next * damp
-        gain = 2.0 * damp_next / half_width
         for g in range(GROUPS):
             prod = jnp.dot(stacked[g], right, preferred_element_type=f32)
             for first in range(0, rows, 8):
@@ -263,9 +256,20 @@
                     new = keep * update[part, cut] + gain * (left * inv)
                     update[part, cut] = new
                     answer[part, cut] = answer[part, cut] + new
+
+    def step(_, damp):
+        damp_next = 1.0 / (f32(2.0 * sigma) - damp)
+        sweep(damp_next * damp, damp_next * f32(2.0 / 0.45))
         return damp_next
 
-    lax.fori_loop(0, SWEEPS, sweep, damping)
+    if total == LANES:
+        damp = 1.0 / sigma
+        for _ in range(SWEEPS):
+            damp_next = 1.0 / (2.0 * sigma - damp)
+            sweep(f32(damp_next * damp), f32(2.0 * damp_next / 0.45))
+            damp = damp_next
+    else:
+        lax.fori_loop(0, SWEEPS, step, jnp.full((1, 1), 1.0 / sigma, f32))
     grp_count = strides[0] // count
     firsts = total // strides[0]
     half = dof // 2

time: 35.1 us -> 35.1 us (level)
  no operation moved by 1% of the time
where the time goes in v5:
time: 35.1 us; the launch traced here: 34.8 us
  blocking collectives  12.3 us (35%)
  Pallas kernels  9.9 us (28%)
  starting transfers between devices  7.09 us (20%)
  waiting for transfers between devices  5.48 us (16%)
    all_to_all x1, blocking collectives, local(): back = lax.all_to_all(back, every, 0, 0, tiled=True)  12.3 us
    all_to_all x1, starting transfers between devices, local(): lax.all_to_all(sent.reshape(members, 1, (count + 1) * LANES), every, 0, 0...  7.09 us
    all_to_all x1, waiting for transfers between devices, local(): lax.all_to_all(sent.reshape(members, 1, (count + 1) * LANES), every, 0, 0...  5.48 us
    pallas_call x1, Pallas kernels, local(): pl.pallas_call(lambda *refs: solve_kernel(strides, *refs), out_shape=pltp...  4.76 us
    pallas_call x1, Pallas kernels, local(): pl.pallas_call(coarse_kernel, out_shape=(pltpu.HBM((members * (count + 1)...  2.3 us
    pallas_call x1, Pallas kernels, local(): pl.pallas_call(matrices_kernel, out_shape=(pltpu.VMEM((GROUPS, 24 * (dof...  1.93 us
    pallas_call x1, Pallas kernels, local(): pl.pallas_call(finish_kernel, out_shape=jax.ShapeDtypeStruct((slabs * row...  0.91 us
  transfers between devices with their start and end apart: 1, of which 1 were waited for; matrix products, arithmetic and copies ran while one was open for 0% of the time, Pallas kernels for 6%

profile of v5, /device:TPU:1, one launch (start us, length us, event | category | flops | bytes accessed | tf_op | source)
XLA Modules:
  0.0 34.8 jit_solution(17632061365829777302)
XLA Ops:
  0.0 2.3 %coarse.1 = (f32[160,128]{1,0:T(8,128)}, f32[64,64]{1,0:T(8,128)S(1)}, f32[8,64,64]{2,1,0:T(8,128)S(1)}, f32[16,64,64]{2,1,0:T(8,128)S(1)}) custom-call(f32[1,2,2,8]{3,2,1,0:T(2,128)} %dens_h.1, s32[1,2,2,8]{3,2,1,0:T(2,128)} %slot_h.1, s32[1,2,2,6]{3,2,1,0:T(2,128)} %links_h.1, s32[1,2,2,6]{3,2,1,0:T(2,128)} %code_h.1, f32[64,64]{1,0:T(8,128)} %stiffness_h.1, ...), custom_call_target="tpu_custom_call" | custom-call | tf_op jit(solution)/shard_map/coarse/pallas_call | solution.py:324
  2.3 7.1 %all-to-all-start = ((f32[32,1,640]{2,1,0:T(1,128)}), f32[32,1,640]{2,1,0:T(1,128)S(1)}, u32[]{:S(2)}, u32[]{:S(2)}) async-start(f32[32,1,640]{2,1,0:T(1,128)} %bitcast.8), calls=%async_computation | async-start | bytes 163840 | tf_op jit(solution)/shard_map/all_to_all | solution.py:355
  9.4 1.9 %matrices.1 = (bf16[4,384,192]{2,1,0:T(8,128)(2,1)S(1)}, bf16[17,128,192]{2,1,0:T(8,128)(2,1)S(1)}) custom-call(f32[64,64]{1,0:T(8,128)S(1)} %get-tuple-element.12.stiffness, f32[8,64,64]{2,1,0:T(8,128)S(1)} %get-tuple-element.13.prolong, f32[16,64,64]{2,1,0:T(8,128)S(1)} %get-tuple-element.14.penalty), custom_call_target="tpu_custom_call" | custom-call | tf_op jit(solution)/shard_map/matrices/pallas_call | solution.py:357
  11.3 5.5 %all-to-all-done = f32[32,1,640]{2,1,0:T(1,128)S(1)} async-done(((f32[32,1,640]{2,1,0:T(1,128)}), f32[32,1,640]{2,1,0:T(1,128)S(1)}, u32[]{:S(2)}, u32[]{:S(2)}) %all-to-all-start) | async-done | bytes 81952 | tf_op jit(solution)/shard_map/all_to_all | solution.py:355
  16.8 4.8 %solve.1 = f32[32,16,128]{2,1,0:T(8,128)S(1)} custom-call(f32[160,128]{1,0:T(8,128)S(1)} %bitcast.7, bf16[4,384,192]{2,1,0:T(8,128)(2,1)S(1)} %get-tuple-element.15.refs_1_, bf16[17,128,192]{2,1,0:T(8,128)(2,1)S(1)} %get-tuple-element.16.refs_2_), custom_call_target="tpu_custom_call" | custom-call | tf_op jit(solution)/shard_map/solve/pallas_call | solution.py:369
  21.6 12.3 %all_to_all.10.got = f32[32,16,128]{2,1,0:T(8,128)S(1)} all-to-all(f32[32,16,128]{2,1,0:T(8,128)S(1)} %solve.1), channel_id=1, replica_groups=mesh['slab'=4,'grp'=8] {'slab','grp'}, dimensions={0} | all-to-all | bytes 524288 | tf_op jit(solution)/shard_map/all_to_all | solution.py:384
  33.9 0.9 %finish.1 = f32[8,64,128]{2,1,0:T(8,128)} custom-call(f32[32,16,128]{2,1,0:T(8,128)S(1)} %all_to_all.10.got), custom_call_target="tpu_custom_call" | custom-call | tf_op jit(solution)/shard_map/finish/pallas_call | solution.py:385
Async XLA Ops:
  2.3 14.5 %all-to-all-start = ((f32[32,1,640]{2,1,0:T(1,128)}), f32[32,1,640]{2,1,0:T(1,128)S(1)}, u32[]{:S(2)}, u32[]{:S(2)}) async-start(f32[32,1,640]{2,1,0:T(1,128)} %bitcast.8), calls=%async_computation | async-start | bytes 163840 | tf_op jit(solution)/shard_map/all_to_all | solution.py:355
